TPU v7x, 512 devices: a whole 4x4x16 slice. The times are simulated.
512 devices in a mesh: ctx: 16 (over x, z_hi, core), ch: 32 (over z_lo, y).
Axes of the slice: x: 4, y: 4, z: 16 (z_hi: 2, z_lo: 8; z = z_hi * 8 + z_lo), core: 2. Of those that a mesh axis runs over, the one named last changes fastest.
Arguments:
- query_gate: bfloat16 [4096, 8192], P(('ctx', 'ch')), may hold values from -6 to 6
- key_gate: bfloat16 [4096, 8192], P(('ctx', 'ch')), may hold values from -6 to 6
- value_proj: bfloat16 [4096, 8192], P(('ctx', 'ch')), may hold values from -6 to 6
- grad_out: bfloat16 [4096, 8192], P(('ctx', 'ch')), may hold values from -0.375 to 0.375
- long_filters: float32 [512, 4096], P('ch', 'ctx'), may hold values from -0.09375 to 0.09375
Outputs:
- grad_query: bfloat16 [4096, 8192], P(('ctx', 'ch'))
- grad_key: bfloat16 [4096, 8192], P(('ctx', 'ch'))
- grad_value: bfloat16 [4096, 8192], P(('ctx', 'ch'))
- grad_filters: float32 [512, 4096], P('ch', 'ctx')
All inputs are finite; a program needn't handle non-finite values.
Results may differ from a plain program's by a relative error of at most 0.0058.
Values may be sent and summed in bfloat16 or wider, within the bound.
No kernel may reach another device: no remote copies, remote signals or barrier semaphores. Data moves between devices by JAX's collectives and lax.ppermute only.
A program may use at most 64 MiB of HBM per device.

v0:
```python
import math

import jax
import jax.numpy as jnp
from jax import lax
from jax.sharding import PartitionSpec as P

GROUP_CH = 16


HIGHEST_MODE = lax.Precision.HIGHEST
SPLIT_MODE = lax.Precision.HIGH


def passed_along(value, axis, steps):
    count = lax.axis_size(axis)
    leading, last = (max(0, -steps), min(count, count - steps))
    return lax.ppermute(value, axis, [(source, source + steps) for source in range(leading, last)])


def make_tables(block_len):
    period = 2 * block_len
    steps = lax.iota(jnp.int32, block_len)
    phase = steps[:, None] * steps[None, :] % period
    angle = phase.astype(jnp.float32) * (math.pi / block_len)
    cosine = jnp.cos(angle)
    sine = jnp.sin(angle)
    parity = 1.0 - 2.0 * (steps % 2).astype(jnp.float32)
    weights = jnp.where(steps == 0, 1.0, 2.0).astype(jnp.float32) / period
    return (
        cosine,
        -sine,
        parity,
        cosine * weights[None, :],
        -sine * weights[None, :],
        parity / period,
    )


def columns_forward(tables, values):
    return (
        jnp.dot(tables[0], values, precision=SPLIT_MODE),
        jnp.dot(tables[1], values, precision=SPLIT_MODE),
        jnp.dot(tables[2], values, precision=SPLIT_MODE),
    )


def columns_inverse(tables, real_part, imag_part, nyquist):
    return (
        jnp.dot(tables[3], real_part, precision=SPLIT_MODE)
        + jnp.dot(tables[4], imag_part, precision=SPLIT_MODE)
        + tables[5][:, None] * nyquist[None, :]
    )


def rows_forward(tables, values):
    return (
        jnp.dot(values, tables[0], precision=HIGHEST_MODE),
        jnp.dot(values, tables[1], precision=HIGHEST_MODE),
        jnp.dot(values, tables[2], precision=HIGHEST_MODE),
    )


def rows_inverse(tables, real_part, imag_part, nyquist):
    return (
        jnp.dot(real_part, tables[3].T, precision=SPLIT_MODE)
        + jnp.dot(imag_part, tables[4].T, precision=SPLIT_MODE)
        + nyquist[:, None] * tables[5][None, :]
    )


def spread_groups(rows):
    groups, block_len = rows.shape
    return jnp.broadcast_to(rows.T[:, :, None], (block_len, groups, GROUP_CH)).reshape(
        block_len, groups * GROUP_CH
    )


def spread_vector(vector):
    return jnp.broadcast_to(vector[:, None], (vector.shape[0], GROUP_CH)).reshape(-1)


def group_rows(matrix):
    block_len, chans = matrix.shape
    return matrix.reshape(block_len, chans // GROUP_CH, GROUP_CH).sum(axis=2).T


def group_vector(vector):
    return vector.reshape(-1, GROUP_CH).sum(axis=1)


def by_blocks(tables, signal, upstream, long_filters):
    block_len, chans = signal.shape
    groups = long_filters.shape[0]
    nblocks = lax.axis_size("ctx")
    own_block = lax.axis_index("ctx")
    parity = tables[2]
    prev_taps = passed_along(long_filters, "ctx", 1)
    both_re, both_im, both_ny = rows_forward(
        tables, jnp.concatenate([prev_taps, long_filters], axis=0)
    )
    own_re = both_re[:groups] + both_re[groups:] * parity
    own_im = both_im[:groups] + both_im[groups:] * parity
    own_ny = both_ny[:groups] + both_ny[groups:]
    lag_re, lag_im, lag_ny = (
        lax.all_gather(own_re[None], "ctx", axis=0, tiled=True),
        lax.all_gather(own_im[None], "ctx", axis=0, tiled=True),
        lax.all_gather(own_ny[None], "ctx", axis=0, tiled=True),
    )
    mine_re, mine_im, mine_ny = columns_forward(tables, upstream.astype(jnp.float32))
    mine_re = mine_re * parity[:, None]
    mine_im = mine_im * parity[:, None]

    def pick(lag_index):
        return (
            spread_groups(lax.dynamic_index_in_dim(lag_re, lag_index, 0, keepdims=False)),
            spread_groups(lax.dynamic_index_in_dim(lag_im, lag_index, 0, keepdims=False)),
            spread_vector(lax.dynamic_index_in_dim(lag_ny, lag_index, 0, keepdims=False)),
        )

    def add_earlier(totals, block_vals, lag_index):
        conv_re, conv_im, conv_ny, back_re, back_im, back_ny, corr_re, corr_im, corr_ny = totals
        sig_re, sig_im, sig_ny = columns_forward(tables, block_vals)
        tap_re, tap_im, tap_ny = pick(lag_index)
        conv_re = conv_re + tap_re * sig_re - tap_im * sig_im
        conv_im = conv_im + tap_re * sig_im + tap_im * sig_re
        conv_ny = conv_ny + tap_ny * sig_ny
        corr_re = corr_re.at[lag_index].add(group_rows(mine_re * sig_re + mine_im * sig_im))
        corr_im = corr_im.at[lag_index].add(group_rows(mine_im * sig_re - mine_re * sig_im))
        corr_ny = corr_ny.at[lag_index].add(group_vector(mine_ny * sig_ny))
        return (conv_re, conv_im, conv_ny, back_re, back_im, back_ny, corr_re, corr_im, corr_ny)

    def add_later(totals, block_vals, lag_index):
        conv_re, conv_im, conv_ny, back_re, back_im, back_ny, corr_re, corr_im, corr_ny = totals
        up_re, up_im, up_ny = columns_forward(tables, block_vals)
        up_re = up_re * parity[:, None]
        up_im = up_im * parity[:, None]
        tap_re, tap_im, tap_ny = pick(lag_index)
        back_re = back_re + tap_re * up_re + tap_im * up_im
        back_im = back_im + tap_re * up_im - tap_im * up_re
        back_ny = back_ny + tap_ny * up_ny
        return (conv_re, conv_im, conv_ny, back_re, back_im, back_ny, corr_re, corr_im, corr_ny)

    plane = jnp.zeros((block_len, chans), jnp.float32)
    edge = jnp.zeros((chans,), jnp.float32)
    stack = jnp.zeros((nblocks, groups, block_len), jnp.float32)
    stack_edge = jnp.zeros((nblocks, groups), jnp.float32)
    initial = (plane, plane, edge, plane, plane, edge, stack, stack, stack_edge)
    sig_piece = lax.all_gather(signal, "ctx", axis=0, tiled=True)
    up_piece = lax.all_gather(upstream, "ctx", axis=0, tiled=True)
    piece_blocks = sig_piece.shape[0] // block_len

    def one_block(offset, running):
        sig_vals = lax.dynamic_slice_in_dim(sig_piece, offset * block_len, block_len, 0).astype(
            jnp.float32
        )
        up_vals = lax.dynamic_slice_in_dim(up_piece, offset * block_len, block_len, 0).astype(
            jnp.float32
        )
        running = lax.cond(
            offset <= own_block,
            lambda current: add_earlier(current, sig_vals, own_block - offset),
            lambda current: current,
            running,
        )
        running = lax.cond(
            offset >= own_block,
            lambda current: add_later(current, up_vals, offset - own_block),
            lambda current: current,
            running,
        )
        return running

    totals = lax.fori_loop(0, piece_blocks, one_block, initial)
    conv_re, conv_im, conv_ny, back_re, back_im, back_ny, corr_re, corr_im, corr_ny = totals
    convolved = columns_inverse(
        tables, conv_re * parity[:, None], conv_im * parity[:, None], conv_ny
    )
    correlated = columns_inverse(tables, back_re, back_im, back_ny)
    total_re, total_im, total_ny = lax.psum((corr_re, corr_im, corr_ny), "ctx")
    next_block = jnp.minimum(own_block + 1, nblocks - 1)
    valid = (own_block + 1 < nblocks).astype(jnp.float32)
    cur_re = lax.dynamic_index_in_dim(total_re, own_block, 0, keepdims=False)
    cur_im = lax.dynamic_index_in_dim(total_im, own_block, 0, keepdims=False)
    cur_ny = lax.dynamic_index_in_dim(total_ny, own_block, 0, keepdims=False)
    nxt_re = lax.dynamic_index_in_dim(total_re, next_block, 0, keepdims=False)
    nxt_im = lax.dynamic_index_in_dim(total_im, next_block, 0, keepdims=False)
    nxt_ny = lax.dynamic_index_in_dim(total_ny, next_block, 0, keepdims=False)
    upper = rows_inverse(tables, cur_re * parity, cur_im * parity, cur_ny)
    lower = rows_inverse(tables, nxt_re, nxt_im, nxt_ny)
    grad_filters = upper + lower * valid
    return (convolved, correlated, grad_filters)


def on_device(query_gate, key_gate, value_proj, grad_out, long_filters):
    query_cols, key_cols, value_cols, grad_cols = (
        lax.all_to_all(query_gate, "ch", split_axis=1, concat_axis=0, tiled=True),
        lax.all_to_all(key_gate, "ch", split_axis=1, concat_axis=0, tiled=True),
        lax.all_to_all(value_proj, "ch", split_axis=1, concat_axis=0, tiled=True),
        lax.all_to_all(grad_out, "ch", split_axis=1, concat_axis=0, tiled=True),
    )
    query_vals = query_cols.astype(jnp.float32)
    key_vals = key_cols.astype(jnp.float32)
    value_vals = value_cols.astype(jnp.float32)
    grad_vals = grad_cols.astype(jnp.float32)
    signal = (key_vals * value_vals).astype(jnp.bfloat16)
    upstream = (grad_vals * query_vals).astype(jnp.bfloat16)
    tables = make_tables(signal.shape[0])
    convolved, correlated, grad_filters = by_blocks(tables, signal, upstream, long_filters)
    conv_half = convolved.astype(jnp.bfloat16)
    corr_half = correlated.astype(jnp.bfloat16)
    conv_wide = lax.optimization_barrier(conv_half).astype(jnp.float32)
    corr_wide = lax.optimization_barrier(corr_half).astype(jnp.float32)
    grad_query = (grad_vals * conv_wide).astype(jnp.bfloat16)
    grad_key = (corr_wide * value_vals).astype(jnp.bfloat16)
    grad_value = (corr_wide * key_vals).astype(jnp.bfloat16)
    query_rows, key_rows, value_rows = (
        lax.all_to_all(grad_query, "ch", split_axis=0, concat_axis=1, tiled=True),
        lax.all_to_all(grad_key, "ch", split_axis=0, concat_axis=1, tiled=True),
        lax.all_to_all(grad_value, "ch", split_axis=0, concat_axis=1, tiled=True),
    )
    return (query_rows, key_rows, value_rows, grad_filters)


def solution(mesh):
    in_specs = (
        P(("ctx", "ch"), None),
        P(("ctx", "ch"), None),
        P(("ctx", "ch"), None),
        P(("ctx", "ch"), None),
        P("ch", "ctx"),
    )
    out_specs = (
        P(("ctx", "ch"), None),
        P(("ctx", "ch"), None),
        P(("ctx", "ch"), None),
        P("ch", "ctx"),
    )
    return jax.shard_map(
        on_device, mesh=mesh, in_specs=in_specs, out_specs=out_specs, check_vma=False
    )
```

profile of v0, /device:TPU:1, one launch (start us, length us, event | category | flops | bytes accessed | tf_op | source)
XLA Modules:
  0.0 772.2 jit_solution(13304330586870944994)
XLA Ops:
  7.2 28.2 %all_to_all.109 = bf16[8,32,256]{2,0,1:T(8,128)(2,1)S(1)} all-to-all(bf16[8,32,256]{2,0,1:T(8,128)(2,1)} %bitcast.162), channel_id=1, replica_groups=mesh['ctx'=16,'ch'=32] {'ch'}, dimensions={1} | all-to-all | bytes 262144 | tf_op jit(solution)/shard_map/all_to_all | solution.py:200
  35.4 18.9 %all_to_all.110 = bf16[8,32,256]{2,0,1:T(8,128)(2,1)S(1)} all-to-all(bf16[8,32,256]{2,0,1:T(8,128)(2,1)} %bitcast.163), channel_id=1, replica_groups=mesh['ctx'=16,'ch'=32] {'ch'}, dimensions={1} | all-to-all | bytes 262144 | tf_op jit(solution)/shard_map/all_to_all | solution.py:197
  55.1 18.8 %all_to_all.111 = bf16[8,32,256]{2,0,1:T(8,128)(2,1)S(1)} all-to-all(bf16[8,32,256]{2,0,1:T(8,128)(2,1)} %bitcast.164), channel_id=1, replica_groups=mesh['ctx'=16,'ch'=32] {'ch'}, dimensions={1} | all-to-all | bytes 262144 | tf_op jit(solution)/shard_map/all_to_all | solution.py:198
  73.8 18.7 %all_to_all.112 = bf16[8,32,256]{2,0,1:T(8,128)(2,1)S(1)} all-to-all(bf16[8,32,256]{2,0,1:T(8,128)(2,1)} %bitcast.165), channel_id=1, replica_groups=mesh['ctx'=16,'ch'=32] {'ch'}, dimensions={1} | all-to-all | bytes 262144 | tf_op jit(solution)/shard_map/all_to_all | solution.py:199
  93.9 11.1 %collective-permute-start = (f32[16,256]{1,0:T(8,128)S(1)}, f32[16,256]{1,0:T(8,128)S(1)}, u32[]{:S(2)}, u32[]{:S(2)}) collective-permute-start(f32[16,256]{1,0:T(8,128)S(1)} %copy-done.6), channel_id=1, source_target_pairs={{0,32},{32,64},{64,96},{96,128},{128,160},{160,192},{192,224},{224... | collective-permute-start | bytes 49160 | tf_op jit(solution)/shard_map/ppermute | solution.py:18
  106.3 1.3 dynamic-slice.32
  108.5 76.4 %all-reduce = f32[256]{0:T(256)S(1)} all-reduce(f32[256]{0:T(256)S(1)} %add_dynamic-update-slice_fusion), channel_id=4, replica_groups=mesh['ctx'=16,'ch'=32] {'ctx'}, use_global_device_ids=true, to_apply=%add | all-reduce | flops 256 | bytes 2048
  186.8 1.2 fusion.78
  188.0 58.5 %all-gather = f32[256,256]{1,0:T(8,128)} all-gather(f32[16,256]{1,0:T(8,128)S(1)} %get-tuple-element.813), channel_id=2, replica_groups=mesh['ctx'=16,'ch'=32] {'ctx'}, dimensions={0}, use_global_device_ids=true | all-gather | bytes 278528 | tf_op jit(solution)/shard_map/all_gather | solution.py:106
  246.6 36.5 %all-gather.1 = f32[256,256]{1,0:T(8,128)} all-gather(f32[16,256]{1,0:T(8,128)S(1)} %get-tuple-element.812), channel_id=3, replica_groups=mesh['ctx'=16,'ch'=32] {'ctx'}, dimensions={0}, use_global_device_ids=true | all-gather | bytes 278528 | tf_op jit(solution)/shard_map/all_gather | solution.py:107
  283.1 1.3 convolution_multiply_fusion.3
  284.5 1.3 convolution_multiply_fusion.2
  288.1 112.7 %while.34 = (s32[]{:T(128)}, f32[256,256]{0,1:T(8,128)S(1)}, f32[256,256]{0,1:T(8,128)S(1)}, f32[256]{0:T(256)}, f32[256,256]{1,0:T(8,128)S(1)}, /*index=5*/f32[...) while((s32[]{:T(128)}, f32[256,256]{0,1:T(8,128)S(1)}, ...), condition=%wide.region_10.11_spmd.clone.clone, body=%wide.region_0.10_spmd.clone.clone.sunk | while | flops 406269760 | bytes 10842854 | solution.py:174
  290.2 8.9 %conditional.8 = ((f32[256,256]{0,1:T(8,128)S(1)}, f32[256,256]{0,1:T(8,128)S(1)}, f32[256]{0:T(256)}, f32[16,16,256]{2,1,0:T(8,128)S(1)}, f32[16,16,256]{2,1,0:T(8,128)}, /*index=5*/f32[16,16]{1,0:T(8,128)S(1)})) conditional(s32[]{:T(128)} %convert_element_type.338, (f32[256,256]{0,1:T(8,128)S(1)}, f32[256,256]{0,1:T(8,128)S(1)}, f32[256]{0:T(256)}, ...), branch_computations={%region_1.1_spmd, %region_2.7_spmd} | conditional | flops 202777648 | bytes 4439917 | solution.py:160
  293.4 1.9 fusion.10
  296.3 1.3 fusion.143
  301.3 8.9 %conditional.8 = ((f32[256,256]{0,1:T(8,128)S(1)}, f32[256,256]{0,1:T(8,128)S(1)}, f32[256]{0:T(256)}, f32[16,16,256]{2,1,0:T(8,128)S(1)}, f32[16,16,256]{2,1,0:T(8,128)}, /*index=5*/f32[16,16]{1,0:T(8,128)S(1)})) conditional(s32[]{:T(128)} %convert_element_type.338, (f32[256,256]{0,1:T(8,128)S(1)}, f32[256,256]{0,1:T(8,128)S(1)}, f32[256]{0:T(256)}, ...), branch_computations={%region_1.1_spmd, %region_2.7_spmd} | conditional | flops 202777648 | bytes 4439917 | solution.py:160
  304.5 1.9 fusion.10
  307.3 1.3 fusion.143
  310.2 4.1 conditional.9
  313.0 1.3 multiply_add_fusion.3
  316.4 4.1 conditional.9
  319.2 1.3 multiply_add_fusion.3
  322.6 4.1 conditional.9
  325.4 1.3 multiply_add_fusion.3
  328.8 4.1 conditional.9
  331.5 1.3 multiply_add_fusion.3
  334.9 4.1 conditional.9
  337.7 1.3 multiply_add_fusion.3
  341.1 4.1 conditional.9
  343.9 1.3 multiply_add_fusion.3
  347.3 4.1 conditional.9
  350.1 1.3 multiply_add_fusion.3
  353.5 4.1 conditional.9
  356.3 1.3 multiply_add_fusion.3
  359.7 4.1 conditional.9
  362.4 1.3 multiply_add_fusion.3
  365.8 4.1 conditional.9
  368.6 1.3 multiply_add_fusion.3
  372.0 4.1 conditional.9
  374.8 1.3 multiply_add_fusion.3
  378.2 4.1 conditional.9
  381.0 1.3 multiply_add_fusion.3
  384.4 4.1 conditional.9
  387.2 1.3 multiply_add_fusion.3
  390.6 4.1 conditional.9
  393.3 1.3 multiply_add_fusion.3
  396.7 4.1 conditional.9
  399.5 1.3 multiply_add_fusion.3
  400.8 2.0 fusion.54
  402.9 1.9 fusion.27
  405.6 3.9 all-to-all-start.5
  409.6 12.0 %all-to-all-done.5 = bf16[32,8,256]{2,1,0:T(8,128)(2,1)S(1)} async-done(((bf16[32,8,256]{2,1,0:T(8,128)(2,1)}), bf16[32,8,256]{2,1,0:T(8,128)(2,1)S(1)}, u32[]{:S(2)}, u32[]{:S(2)}) %all-to-all-start.5) | async-done | bytes 131104 | tf_op jit(solution)/shard_map/all_to_all | solution.py:219
  421.6 4.3 all-to-all-start.6
  425.9 1.2 fusion.41
  427.3 1.9 fusion.26
  430.0 8.0 %all-to-all-done.6 = bf16[32,8,256]{2,1,0:T(8,128)(2,1)S(1)} async-done(((bf16[32,8,256]{2,1,0:T(8,128)(2,1)}), bf16[32,8,256]{2,1,0:T(8,128)(2,1)S(1)}, u32[]{:S(2)}, u32[]{:S(2)}) %all-to-all-start.6) | async-done | bytes 131104 | tf_op jit(solution)/shard_map/all_to_all | solution.py:220
  438.0 4.3 all-to-all-start.4
  442.3 128.9 %psum.23 = f32[16,16]{1,0:T(8,128)S(1)} all-reduce(f32[16,16]{1,0:T(8,128)S(1)} %get-tuple-element.559), channel_id=1, replica_groups=mesh['ctx'=16,'ch'=32] {'ctx'}, use_global_device_ids=true, to_apply=%region_13.14 | all-reduce | flops 256 | bytes 2048 | tf_op jit(solution)/shard_map/psum | solution.py:180
  571.2 184.2 %all-reduce.4.cloned.1.call-done = (f32[16,16,256]{2,1,0:T(8,128)}, f32[16,16,256]{2,1,0:T(8,128)}) async-done(((f32[16,16,256]{2,1,0:T(8,128)}, f32[16,16,256]{2,1,0:T(8,128)}), (f32[16,16,256]{2,1,0:T(8,128)}, f32[16,16,256]{2,1,0:T(8,128)})) %all-reduce.4.cloned.1.call-update) | async-done | bytes 524304 | tf_op jit(solution)/shard_map/psum | solution.py:180
  755.5 1.8 fusion.52
  757.3 1.9 fusion.50
  759.2 1.9 fusion.31
  761.1 2.6 fusion.30
  (331 shorter events, 96.9 us)
Async XLA Ops:
  7.2 86.8 %copy-start.6 = (f32[16,256]{1,0:T(8,128)S(1)}, f32[16,256]{1,0:T(8,128)}, u32[]{:S(2)}) copy-start(f32[16,256]{1,0:T(8,128)} %param.21) | copy-start | bytes 49156
  7.2 278.9 %all-gather.8.cloned.1.call-start = ((), (), s32[]{:S(2)}) async-start(), calls=%async_computation.8 | async-start | bytes 2228224 | tf_op jit(solution)/shard_map/all_gather | solution.py:150
  55.0 228.1 %copy-start.5 = (bf16[256,256]{1,0:T(8,128)(2,1)S(1)}, bf16[256,256]{1,0:T(8,128)(2,1)}, u32[]{:S(2)}) copy-start(bf16[256,256]{1,0:T(8,128)(2,1)} %fusion.37) | copy-start | bytes 393220
  55.0 231.0 %all-gather.6.cloned.1.call-start = ((), (), s32[]{:S(2)}) async-start(), calls=%async_computation.7 | async-start | bytes 2228224 | tf_op jit(solution)/shard_map/all_gather | solution.py:149
  73.8 18.7 %copy-start.1 = (bf16[8,32,256]{2,0,1:T(8,128)(2,1)}, bf16[8,32,256]{2,0,1:T(8,128)(2,1)S(1)}, u32[]{:S(2)}) copy-start(bf16[8,32,256]{2,0,1:T(8,128)(2,1)S(1)} %all_to_all.111) | copy-start | bytes 393220
  92.5 0.7 copy-start.3
  93.9 14.3 %collective-permute-start = (f32[16,256]{1,0:T(8,128)S(1)}, f32[16,256]{1,0:T(8,128)S(1)}, u32[]{:S(2)}, u32[]{:S(2)}) collective-permute-start(f32[16,256]{1,0:T(8,128)S(1)} %copy-done.6), channel_id=1, source_target_pairs={{0,32},{32,64},{64,96},{96,128},{128,160},{160,192},{192,224},{224... | collective-permute-start | bytes 49160 | tf_op jit(solution)/shard_map/ppermute | solution.py:18
  105.1 180.8 %copy-start.9 = (f32[256]{0:T(256)}, f32[256]{0:T(256)S(1)}, u32[]{:S(2)}) copy-start(f32[256]{0:T(256)S(1)} %fusion.104) | copy-start | bytes 3076
  290.2 2.5 copy-start.8
  291.6 6.1 copy-start.7
  301.3 2.5 copy-start.8
  302.7 6.1 copy-start.7
  400.8 20.7 %copy-start = (f32[16,16,256]{2,1,0:T(8,128)}, f32[16,16,256]{2,1,0:T(8,128)S(1)}, u32[]{:S(2)}) copy-start(f32[16,16,256]{2,1,0:T(8,128)S(1)} %get-tuple-element.557) | copy-start | bytes 786436
  400.8 4.0 copy-start.2
  400.8 4.0 copy-start.4
  400.8 25.1 %copy-start.10 = (f32[256]{0:T(256)S(1)}, f32[256]{0:T(256)}, u32[]{:S(2)}) copy-start(f32[256]{0:T(256)} %copy-done.9) | copy-start | bytes 3076
  400.8 25.1 %copy-start.11 = (f32[256]{0:T(256)S(1)}, f32[256]{0:T(256)}, u32[]{:S(2)}) copy-start(f32[256]{0:T(256)} %fusion.101) | copy-start | bytes 3076
  404.8 22.5 %copy-start.12 = (f32[256]{0:T(256)S(1)}, f32[256]{0:T(256)}, u32[]{:S(2)}) copy-start(f32[256]{0:T(256)} %broadcast_multiply_fusion) | copy-start | bytes 3076
  405.6 16.0 %all-to-all-start.5 = ((bf16[32,8,256]{2,1,0:T(8,128)(2,1)}), bf16[32,8,256]{2,1,0:T(8,128)(2,1)S(1)}, u32[]{:S(2)}, u32[]{:S(2)}) async-start(bf16[32,8,256]{2,1,0:T(8,128)(2,1)} %get-tuple-element.809), calls=%async_computation.5 | async-start | bytes 262144 | tf_op jit(solution)/shard_map/all_to_all | solution.py:219
  421.6 16.4 %all-to-all-start.6 = ((bf16[32,8,256]{2,1,0:T(8,128)(2,1)}), bf16[32,8,256]{2,1,0:T(8,128)(2,1)S(1)}, u32[]{:S(2)}, u32[]{:S(2)}) async-start(bf16[32,8,256]{2,1,0:T(8,128)(2,1)} %get-tuple-element.808), calls=%async_computation.6 | async-start | bytes 262144 | tf_op jit(solution)/shard_map/all_to_all | solution.py:220
  425.9 329.6 %all-reduce.4.cloned.1.call-start = ((), (), s32[]{:S(2)}) async-start(), calls=%async_computation.9 | async-start | bytes 1048576 | tf_op jit(solution)/shard_map/psum | solution.py:180
  438.0 133.2 %all-to-all-start.4 = ((bf16[32,8,256]{2,1,0:T(8,128)(2,1)}), bf16[32,8,256]{2,1,0:T(8,128)(2,1)S(1)}, u32[]{:S(2)}, u32[]{:S(2)}) async-start(bf16[32,8,256]{2,1,0:T(8,128)(2,1)} %fusion.57), calls=%async_computation.4 | async-start | bytes 262144 | tf_op jit(solution)/shard_map/all_to_all | solution.py:218
Sparse Core Ops, SparseCore 0:
  55.1 90.3 all-gather.7
  149.4 86.3 all-gather.5
  429.6 325.7 all-reduce.3
where the time goes:
time: 779 us; the launch traced here: 772 us
  blocking collectives  385 us (49%)
  waiting for transfers between devices  204 us (26%)
  other arithmetic  67.5 us (9%)
  local copies, waits for them, and re-layouts  40.3 us (5%)
  matrix products  34.9 us (4%)
  starting transfers between devices  23.7 us (3%)
  between operations  14.7 us (2%)
    psum x1, waiting for transfers between devices, by_blocks(): total_re, total_im, total_ny = lax.psum((corr_re, corr_im, corr_ny), 'ctx')  184 us
    psum x1, blocking collectives, by_blocks(): total_re, total_im, total_ny = lax.psum((corr_re, corr_im, corr_ny), 'ctx')  129 us
    unnamed x1, blocking collectives  76.4 us
    all_gather x1, blocking collectives, by_blocks(): lax.all_gather(own_re[None], 'ctx', axis=0, tiled=True)  58.5 us
    all_gather x1, blocking collectives, by_blocks(): lax.all_gather(own_im[None], 'ctx', axis=0, tiled=True)  36.5 us
    all_to_all x1, blocking collectives, on_device(): lax.all_to_all(grad_out, 'ch', split_axis=1, concat_axis=0, tiled=True)  28.2 us
    add x15, other arithmetic, add_later(): back_ny = back_ny + tap_ny * up_ny  19.4 us
    all_to_all x1, blocking collectives, on_device(): lax.all_to_all(query_gate, 'ch', split_axis=1, concat_axis=0, tiled=True)  18.9 us
  transfers between devices with their start and end apart: 7, of which 3 were waited for; matrix products, arithmetic and copies ran while one was open for 2% of the time, Pallas kernels for 0%

commit v1 on v0

v1 whole, which is shorter than its diff:
```python
import jax
import jax.numpy as jnp
from jax import lax
from jax.experimental import pallas as pl
from jax.experimental.pallas import tpu as pltpu
from jax.sharding import PartitionSpec as P

CH = 16
TOK = 8
ROWS = 128
F32 = jnp.float32
BF16 = jnp.bfloat16


def lane_of(shape):
    return lax.broadcasted_iota(jnp.int32, shape, 1)


def row_of(shape):
    return lax.broadcasted_iota(jnp.int32, shape, 0)


def swap_segments(x):
    row, seg = row_of(x.shape), lane_of(x.shape) // CH
    for bit in range(3):
        step = 1 << bit
        row_bit, seg_bit = (row >> bit) & 1, (seg >> bit) & 1
        down = pltpu.roll(pltpu.roll(x, step, 0), 128 - CH * step, 1)
        up = pltpu.roll(pltpu.roll(x, TOK - step, 0), CH * step, 1)
        x = jnp.where(row_bit == seg_bit, x, jnp.where(row_bit == 1, down, up))
    return x


def pack_kernel(q_ref, k_ref, v_ref, g_ref, o_ref, wide):
    for block in range(q_ref.shape[1] // 128):
        j, half = divmod(block, 2)
        lanes = pl.ds(block * 128, 128)
        for a, (x_ref, y_ref) in enumerate(((k_ref, v_ref), (g_ref, q_ref))):
            prod = (x_ref[:, lanes].astype(F32) * y_ref[:, lanes].astype(F32)).astype(BF16)
            wide[pl.ds(8 * half * 64 + 2 * j + a, 8, stride=64), :] = swap_segments(prod.astype(F32))
    o_ref[...] = wide[...].astype(BF16)


def unpack_kernel(r_ref, k_ref, v_ref, g_ref, gq_ref, gk_ref, gv_ref, wide):
    wide[...] = r_ref[...].astype(F32)
    for block in range(k_ref.shape[1] // 128):
        j, half = divmod(block, 2)
        lanes = pl.ds(block * 128, 128)
        conv = swap_segments(wide[pl.ds(8 * half * 64 + 2 * j, 8, stride=64), :])
        corr = swap_segments(wide[pl.ds(8 * half * 64 + 2 * j + 1, 8, stride=64), :])
        gq_ref[:, lanes] = (g_ref[:, lanes].astype(F32) * conv).astype(BF16)
        gk_ref[:, lanes] = (corr * v_ref[:, lanes].astype(F32)).astype(BF16)
        gv_ref[:, lanes] = (corr * k_ref[:, lanes].astype(F32)).astype(BF16)


def toeplitz_kernel(h_ref, hi_ref, lo_ref, t_ref, base):
    width = h_ref.shape[1]
    lane8, row8 = lane_of((8, width)), row_of((8, width))
    for p in range(TOK):
        skew = jnp.broadcast_to(h_ref[pl.ds(p, 1), :], (8, width))
        for bit in range(3):
            skew = jnp.where((row8 >> bit) & 1 == 1, pltpu.roll(skew, 1 << bit, 1), skew)
        for r in range(ROWS // 8):
            part = pltpu.roll(skew, 8 * r, 1) if r else skew
            base[pl.ds(8 * r, 8), :] = jnp.where(lane8 >= row8 + 8 * r, part, 0.0)
        whole = base[...]
        high = whole.astype(BF16)
        hi_ref[pl.ds(p * ROWS, ROWS), :] = high
        lo_ref[pl.ds(p * ROWS, ROWS), :] = (whole - high.astype(F32)).astype(BF16)
        for m in range(width // 128):
            flip = whole[:, m * 128 : (m + 1) * 128].T
            high = flip.astype(BF16)
            at = pl.ds(p * width + m * 128, 128)
            t_ref[at, pl.ds(0, 128)] = high
            t_ref[at, pl.ds(128, 128)] = (flip - high.astype(F32)).astype(BF16)


def group_kernel(r_ref, hi_ref, lo_ref, t_ref, o_ref, g_ref, wide, lhs, ahead):
    count = r_ref.shape[0] // 2
    nblk = count // ROWS
    wide[...] = r_ref[...].astype(F32)
    sig = wide[pl.ds(0, count, stride=2), :]
    ups = wide[pl.ds(1, count, stride=2), :]
    sig_t = jnp.concatenate([sig[b * 128 : b * 128 + 128].T for b in range(nblk)], axis=1)
    ups_t = jnp.concatenate([ups[b * 128 : b * 128 + 128].T for b in range(nblk)], axis=1)
    lane = lane_of(sig_t.shape)
    sig_prev = jnp.where(lane == 0, 0.0, pltpu.roll(sig_t, 1, 1)).astype(BF16)
    ups_next = jnp.where(lane == count - 1, 0.0, pltpu.roll(ups_t, count - 1, 1)).astype(BF16)
    sig_t, ups_t = sig_t.astype(BF16), ups_t.astype(BF16)
    for p in range(TOK):
        cut = CH * p
        for b in range(nblk):
            cols = slice(b * 128, b * 128 + 128)
            if p:
                lhs[pl.ds(b * 128, cut), pl.ds(p * 128, 128)] = sig_prev[128 - cut :, cols]
            lhs[pl.ds(b * 128 + cut, 128 - cut), pl.ds(p * 128, 128)] = sig_t[: 128 - cut, cols]
            size = count - 128 * b
            ahead[pl.ds(b * 128, 128 - cut), pl.ds(p * count, size)] = ups_t[cut:, b * 128 :]
            if p:
                ahead[pl.ds(b * 128 + 128 - cut, cut), pl.ds(p * count, size)] = ups_next[:cut, b * 128 :]
            if b:
                ahead[pl.ds(b * 128, 128), pl.ds(p * count + size, 128 * b)] = jnp.zeros((128, 128 * b), BF16)
    conv = [None] * nblk
    for b in range(nblk):
        rows = lhs[pl.ds(b * 128, 128), :]
        size = count - 128 * b
        part = jnp.dot(rows, hi_ref[:, pl.ds(0, size)], preferred_element_type=F32)
        part = part + jnp.dot(rows, lo_ref[:, pl.ds(0, size)], preferred_element_type=F32)
        for k in range(nblk - b):
            piece = part[:, k * 128 : k * 128 + 128]
            conv[b + k] = piece if conv[b + k] is None else conv[b + k] + piece
    back = jnp.dot(ahead[...], t_ref[...], preferred_element_type=F32)
    for b in range(nblk):
        rows = slice(b * 128, b * 128 + 128)
        wide[pl.ds(256 * b, 128, stride=2), :] = conv[b].T
        wide[pl.ds(256 * b + 1, 128, stride=2), :] = (back[rows, :128] + back[rows, 128:]).T
    o_ref[...] = wide[...].astype(BF16)
    side = jnp.concatenate([sig[b * 128 : b * 128 + 128] for b in range(nblk)], axis=1).astype(BF16)
    lane8, row8 = lane_of((8, count)), row_of((8, count))
    for p in range(TOK):
        lags = jnp.dot(side, ahead[:, pl.ds(p * count, count)], preferred_element_type=F32)
        total = jnp.zeros((8, count), F32)
        for r in range(ROWS // 8):
            part = jnp.where(lane8 >= row8 + 8 * r, lags[8 * r : 8 * r + 8], 0.0)
            total = total + (pltpu.roll(part, count - 8 * r, 1) if r else part)
        for bit in range(3):
            total = jnp.where((row8 >> bit) & 1 == 1, pltpu.roll(total, count - (1 << bit), 1), total)
        g_ref[pl.ds(p, 1), :] = jnp.sum(total, axis=0, keepdims=True)


def pack(query, key, value, grad):
    width = query.shape[1]
    rows = 2 * width // CH
    return pl.pallas_call(
        pack_kernel,
        out_shape=jax.ShapeDtypeStruct((rows, 128), BF16),
        scratch_shapes=[pltpu.VMEM((rows, 128), F32)],
        name="pack",
    )(query, key, value, grad)


def unpack(received, key, value, grad):
    shape = jax.ShapeDtypeStruct(key.shape, BF16)
    return pl.pallas_call(
        unpack_kernel,
        out_shape=(shape, shape, shape),
        scratch_shapes=[pltpu.VMEM(received.shape, F32)],
        name="unpack",
    )(received, key, value, grad)


def toeplitz(phases):
    width = phases.shape[1]
    return pl.pallas_call(
        toeplitz_kernel,
        out_shape=(
            jax.ShapeDtypeStruct((TOK * ROWS, width), BF16),
            jax.ShapeDtypeStruct((TOK * ROWS, width), BF16),
            jax.ShapeDtypeStruct((TOK * width, 2 * ROWS), BF16),
        ),
        scratch_shapes=[pltpu.VMEM((ROWS, width), F32)],
        name="toeplitz",
    )(phases)


def group(received, hi, lo, flipped):
    count = received.shape[0] // 2
    return pl.pallas_call(
        group_kernel,
        out_shape=(
            jax.ShapeDtypeStruct(received.shape, BF16),
            jax.ShapeDtypeStruct((TOK, count), F32),
        ),
        scratch_shapes=[
            pltpu.VMEM(received.shape, F32),
            pltpu.VMEM((count, TOK * ROWS), BF16),
            pltpu.VMEM((count, TOK * count), BF16),
        ],
        name="group",
    )(received, hi, lo, flipped)


def exchange(rows):
    pairs = rows.reshape(-1, 2, 128)
    return lax.all_to_all(pairs, ("ctx", "ch"), 0, 0, tiled=True).reshape(rows.shape)


def on_device(query_gate, key_gate, value_proj, grad_out, long_filters):
    groups, taps = long_filters.shape
    fine = taps // TOK
    by_phase = long_filters.reshape(groups, fine, TOK).transpose(0, 2, 1).reshape(groups, taps)
    own = lax.all_to_all(by_phase, "ctx", 0, 0, tiled=True)
    blocks = own.shape[0]
    phases = own.reshape(blocks, TOK, fine).transpose(1, 0, 2).reshape(TOK, blocks * fine)
    received = exchange(pack(query_gate, key_gate, value_proj, grad_out))
    hi, lo, flipped = toeplitz(phases)
    results, lags = group(received, hi, lo, flipped)
    by_block = lags.reshape(TOK, blocks, fine).transpose(1, 0, 2).reshape(blocks, taps)
    home = lax.all_to_all(by_block, "ctx", 0, 0, tiled=True)
    grad_filters = home.reshape(groups, TOK, fine).transpose(0, 2, 1).reshape(groups, taps)
    grads = unpack(exchange(results), key_gate, value_proj, grad_out)
    return (*grads, grad_filters)


def solution(mesh):
    tokens = P(("ctx", "ch"), None)
    return jax.shard_map(
        on_device,
        mesh=mesh,
        in_specs=(tokens, tokens, tokens, tokens, P("ch", "ctx")),
        out_specs=(tokens, tokens, tokens, P("ch", "ctx")),
        check_vma=False,
    )
```

time: 779 us -> 152 us (0.20)
  blocking collectives: 385 us -> 18.6 us
  waiting for transfers between devices: 204 us -> 50.8 us
  other arithmetic: 67.5 us -> 0.08 us
  matrix products: 34.9 us -> 0 us
  local copies, waits for them, and re-layouts: 40.3 us -> 5.59 us
  Pallas kernels: 0 us -> 31.5 us
  starting transfers between devices: 23.7 us -> 43.8 us
  between operations: 14.7 us -> 0.71 us
    psum x1 -> x0, waiting for transfers between devices: 184 us -> none  [by_blocks(): total_re, total_im, total_ny = lax.psum((corr_re, corr_im, corr_ny), 'ctx')]
    psum x1 -> x0, blocking collectives: 129 us -> none  [by_blocks(): total_re, total_im, total_ny = lax.psum((corr_re, corr_im, corr_ny), 'ctx')]
    all_gather x2 -> x0, blocking collectives: 95 us -> none  [the longest x1 58.5 us: by_blocks(): lax.all_gather(own_re[None], 'ctx', axis=0, tiled=True)]
    unnamed x1 -> x0, blocking collectives: 76.4 us -> none
    all_to_all x4 -> x1, blocking collectives: 84.6 us -> 18.6 us  [on_device(): home = lax.all_to_all(by_block, 'ctx', 0, 0, tiled=True)]
    dot_general x65 -> x0, matrix products: 34.9 us -> none  [the longest x18 8.15 us: columns_forward(): jnp.dot(tables[0], values, precision=SPLIT_MODE)]
    pallas_call x0 -> x4, Pallas kernels: none -> 31.5 us  [the longest x1 13.8 us: unpack(): pl.pallas_call(unpack_kernel, out_shape=(shape, shape, shape), scratch_sh...]
    all_to_all x3, starting transfers between devices: 12.5 us -> 43.8 us  [the longest x2 24.8 us: exchange(): lax.all_to_all(pairs, ('ctx', 'ch'), 0, 0, tiled=True).reshape(rows.shape)]
  transfers between devices with their start and end apart: 7 -> 3, of which waited for: 3 -> 3; matrix products, arithmetic and copies ran while one was open for 2% -> 1% of each run, Pallas kernels for 0% -> 7%
where the time goes in v1:
time: 152 us; the launch traced here: 151 us
  waiting for transfers between devices  50.8 us (33%)
  starting transfers between devices  43.8 us (29%)
  Pallas kernels  31.5 us (21%)
  blocking collectives  18.6 us (12%)
  local copies, waits for them, and re-layouts  5.59 us (4%)
    all_to_all x2, waiting for transfers between devices, exchange(): lax.all_to_all(pairs, ('ctx', 'ch'), 0, 0, tiled=True).reshape(rows.shape)  43 us
    all_to_all x2, starting transfers between devices, exchange(): lax.all_to_all(pairs, ('ctx', 'ch'), 0, 0, tiled=True).reshape(rows.shape)  24.8 us
    all_to_all x1, starting transfers between devices, on_device(): own = lax.all_to_all(by_phase, 'ctx', 0, 0, tiled=True)  19.1 us
    all_to_all x1, blocking collectives, on_device(): home = lax.all_to_all(by_block, 'ctx', 0, 0, tiled=True)  18.6 us
    pallas_call x1, Pallas kernels, unpack(): pl.pallas_call(unpack_kernel, out_shape=(shape, shape, shape), scratch_sh...  13.8 us
    all_to_all x1, waiting for transfers between devices, on_device(): own = lax.all_to_all(by_phase, 'ctx', 0, 0, tiled=True)  7.81 us
    pallas_call x1, Pallas kernels, pack(): pl.pallas_call(pack_kernel, out_shape=jax.ShapeDtypeStruct((rows, 128), B...  6.7 us
    pallas_call x1, Pallas kernels, group(): pl.pallas_call(group_kernel, out_shape=(jax.ShapeDtypeStruct(received.sha...  6.47 us
  transfers between devices with their start and end apart: 3, of which 3 were waited for; matrix products, arithmetic and copies ran while one was open for 1% of the time, Pallas kernels for 7%

profile of v1, /device:TPU:1, one launch (start us, length us, event | category | flops | bytes accessed | tf_op | source)
XLA Modules:
  0.0 151.1 jit_solution(12418820771742277420)
XLA Ops:
  0.6 0.8 copy.15
  1.4 0.1 copy.16
  1.6 0.7 all_to_all.24
  2.3 19.1 %all-to-all-start.1 = ((f32[16,1,256]{2,1,0:T(1,128)}), f32[16,1,256]{2,1,0:T(1,128)S(1)}, u32[]{:S(2)}, u32[]{:S(2)}) async-start(f32[16,1,256]{2,1,0:T(1,128)} %all_to_all.24), calls=%async_computation.1 | async-start | bytes 32768 | tf_op jit(solution)/shard_map/all_to_all | solution.py:192
  21.3 6.7 %pack.1 = bf16[1024,128]{1,0:T(8,128)(2,1)} custom-call(bf16[8,8192]{1,0:T(8,128)(2,1)} %q_ref.1, bf16[8,8192]{1,0:T(8,128)(2,1)} %k_ref.3, bf16[8,8192]{1,0:T(8,128)(2,1)} %v_ref.3, bf16[8,8192]{1,0:T(8,128)(2,1)} %g_ref.3), custom_call_target="tpu_custom_call" | custom-call | tf_op jit(solution)/shard_map/pack/pallas_call | solution.py:134
  28.0 7.8 %all-to-all-done.1 = f32[16,1,256]{2,1,0:T(1,128)S(1)} async-done(((f32[16,1,256]{2,1,0:T(1,128)}), f32[16,1,256]{2,1,0:T(1,128)S(1)}, u32[]{:S(2)}, u32[]{:S(2)}) %all-to-all-start.1) | async-done | bytes 16416 | tf_op jit(solution)/shard_map/all_to_all | solution.py:192
  35.8 11.9 %all-to-all-start = ((bf16[512,2,128]{2,1,0:T(2,128)(2,1)}), bf16[512,2,128]{2,1,0:T(2,128)(2,1)S(1)}, u32[]{:S(2)}, u32[]{:S(2)}) async-start(bf16[512,2,128]{2,1,0:T(2,128)(2,1)} %bitcast.14), calls=%async_computation | async-start | bytes 524288 | tf_op jit(solution)/shard_map/all_to_all | solution.py:185
  47.8 0.1 reshape.51
  47.9 0.7 reshape.52.h_ref
  48.5 4.5 %toeplitz.1 = (bf16[1024,512]{1,0:T(8,128)(2,1)}, bf16[1024,512]{1,0:T(8,128)(2,1)}, bf16[4096,256]{1,0:T(8,128)(2,1)}) custom-call(f32[8,512]{1,0:T(8,128)} %reshape.52.h_ref), custom_call_target="tpu_custom_call" | custom-call | tf_op jit(solution)/shard_map/toeplitz/pallas_call | solution.py:154
  53.1 19.3 %all-to-all-done = bf16[512,2,128]{2,1,0:T(2,128)(2,1)S(1)} async-done(((bf16[512,2,128]{2,1,0:T(2,128)(2,1)}), bf16[512,2,128]{2,1,0:T(2,128)(2,1)S(1)}, u32[]{:S(2)}, u32[]{:S(2)}) %all-to-all-start) | async-done | bytes 262176 | tf_op jit(solution)/shard_map/all_to_all | solution.py:185
  72.4 0.0 copy-start
  72.4 0.7 copy-done
  73.1 6.5 %group.1 = (bf16[1024,128]{1,0:T(8,128)(2,1)}, f32[8,512]{1,0:T(8,128)}) custom-call(bf16[1024,128]{1,0:T(8,128)(2,1)} %bitcast.13, bf16[1024,512]{1,0:T(8,128)(2,1)} %get-tuple-element.12.hi_ref, bf16[1024,512]{1,0:T(8,128)(2,1)} %get-tuple-element.13.lo_ref, bf16[4096,256]{1,0:T(8,128)(2,1)} %get-tuple-element.14.t_ref), custom_call_target="tpu_custom_call" | custom-call | tf_op jit(solution)/shard_map/group/pallas_call | solution.py:168
  79.5 0.8 reshape.55
  80.4 0.1 all_to_all.25
  80.5 18.6 %all_to_all.30 = f32[16,1,256]{2,1,0:T(1,128)S(1)} all-to-all(f32[16,1,256]{2,1,0:T(1,128)S(1)} %all_to_all.25), channel_id=1, replica_groups=mesh['ctx'=16,'ch'=32] {'ctx'}, dimensions={0} | all-to-all | bytes 32768 | tf_op jit(solution)/shard_map/all_to_all | solution.py:199
  99.0 12.9 %all-to-all-start.2 = ((bf16[512,2,128]{2,1,0:T(2,128)(2,1)}), bf16[512,2,128]{2,1,0:T(2,128)(2,1)S(1)}, u32[]{:S(2)}, u32[]{:S(2)}) async-start(bf16[512,2,128]{2,1,0:T(2,128)(2,1)} %bitcast.21), calls=%async_computation.2 | async-start | bytes 524288 | tf_op jit(solution)/shard_map/all_to_all | solution.py:185
  112.0 0.1 reshape.56
  112.0 0.1 copy.21
  112.2 0.7 copy.22
  112.9 23.7 %all-to-all-done.2 = bf16[512,2,128]{2,1,0:T(2,128)(2,1)S(1)} async-done(((bf16[512,2,128]{2,1,0:T(2,128)(2,1)}), bf16[512,2,128]{2,1,0:T(2,128)(2,1)S(1)}, u32[]{:S(2)}, u32[]{:S(2)}) %all-to-all-start.2) | async-done | bytes 262176 | tf_op jit(solution)/shard_map/all_to_all | solution.py:185
  136.6 0.0 copy-start.1
  136.6 0.7 copy-done.1
  137.3 13.8 %unpack.1 = (bf16[8,8192]{1,0:T(8,128)(2,1)}, bf16[8,8192]{1,0:T(8,128)(2,1)}, bf16[8,8192]{1,0:T(8,128)(2,1)}) custom-call(bf16[1024,128]{1,0:T(8,128)(2,1)} %bitcast.15, bf16[8,8192]{1,0:T(8,128)(2,1)} %k_ref.3, bf16[8,8192]{1,0:T(8,128)(2,1)} %v_ref.3, bf16[8,8192]{1,0:T(8,128)(2,1)} %g_ref.3), custom_call_target="tpu_custom_call" | custom-call | tf_op jit(solution)/shard_map/unpack/pallas_call | solution.py:144
  (4 shorter events, 0.1 us)
Async XLA Ops:
  2.3 33.6 %all-to-all-start.1 = ((f32[16,1,256]{2,1,0:T(1,128)}), f32[16,1,256]{2,1,0:T(1,128)S(1)}, u32[]{:S(2)}, u32[]{:S(2)}) async-start(f32[16,1,256]{2,1,0:T(1,128)} %all_to_all.24), calls=%async_computation.1 | async-start | bytes 32768 | tf_op jit(solution)/shard_map/all_to_all | solution.py:192
  35.8 36.5 %all-to-all-start = ((bf16[512,2,128]{2,1,0:T(2,128)(2,1)}), bf16[512,2,128]{2,1,0:T(2,128)(2,1)S(1)}, u32[]{:S(2)}, u32[]{:S(2)}) async-start(bf16[512,2,128]{2,1,0:T(2,128)(2,1)} %bitcast.14), calls=%async_computation | async-start | bytes 524288 | tf_op jit(solution)/shard_map/all_to_all | solution.py:185
  72.4 0.7 copy-start
  99.0 37.6 %all-to-all-start.2 = ((bf16[512,2,128]{2,1,0:T(2,128)(2,1)}), bf16[512,2,128]{2,1,0:T(2,128)(2,1)S(1)}, u32[]{:S(2)}, u32[]{:S(2)}) async-start(bf16[512,2,128]{2,1,0:T(2,128)(2,1)} %bitcast.21), calls=%async_computation.2 | async-start | bytes 524288 | tf_op jit(solution)/shard_map/all_to_all | solution.py:185
  136.6 0.7 copy-start.1

commit v2 on v1

v2 whole, which is shorter than its diff:
```python
import jax
import jax.numpy as jnp
from jax import lax
from jax.experimental import pallas as pl
from jax.experimental.pallas import tpu as pltpu
from jax.sharding import Mesh
from jax.sharding import PartitionSpec as P

CH = 16
TOK = 8
ROWS = 128
NX, NZH, NCORE, NZL, NY = 4, 2, 2, 8, 4
NZ = NZH * NZL
NPLANE = NX * NCORE * NY
ZROWS = 2 * NPLANE + 8
PROWS = 2 * NZ + 8
Z_AXES = ("zh", "zl")
PLANE_AXES = ("x", "core", "y")
F32 = jnp.float32
BF16 = jnp.bfloat16


def lane_of(shape):
    return lax.broadcasted_iota(jnp.int32, shape, 1)


def row_of(shape):
    return lax.broadcasted_iota(jnp.int32, shape, 0)


def swap_segments(planes):
    planes = list(planes)
    seg = lane_of(planes[0].shape) // CH
    for bit in range(3):
        step = 1 << bit
        odd = (seg >> bit) & 1 == 1
        for low in range(TOK):
            if low & step:
                continue
            first, second = planes[low], planes[low + step]
            planes[low] = jnp.where(odd, pltpu.roll(second, CH * step, 1), first)
            planes[low + step] = jnp.where(odd, second, pltpu.roll(first, 128 - CH * step, 1))
    return planes


def phase_order(taps, back):
    shape = (taps, taps)
    source, target = row_of(shape), lane_of(shape)
    if back:
        source, target = target, source
    fine = taps // TOK
    return jnp.where((source % TOK) * fine + source // TOK == target, 1.0, 0.0).astype(BF16)


def halves(x):
    high = x.astype(BF16)
    return high, (x - high.astype(F32)).astype(BF16)


def pack_kernel(q_ref, k_ref, v_ref, g_ref, h_ref, o_ref, tile, wide):
    blocks = q_ref.shape[1] // 128
    for a, (x_ref, y_ref) in enumerate(((k_ref, v_ref), (g_ref, q_ref))):
        for block in range(blocks):
            lanes = pl.ds(block * 128, 128)
            prod = (x_ref[:, lanes].astype(F32) * y_ref[:, lanes].astype(F32)).astype(BF16)
            tile[a, pl.ds(block * TOK, TOK), :] = prod.astype(F32)
        for half in range(2):
            planes = [tile[a, pl.ds(half * TOK + t, blocks // 2, stride=2 * TOK), :] for t in range(TOK)]
            for i, plane in enumerate(swap_segments(planes)):
                wide[pl.ds((half * TOK + i) * ZROWS + a, blocks // 2, stride=2), :] = plane
    order = phase_order(h_ref.shape[1], False)
    for n, part in enumerate(halves(h_ref[...])):
        part = jnp.dot(part, order, preferred_element_type=F32)
        for n2 in range(2):
            wide[pl.ds(2 * NPLANE + 2 * n + n2, NZ, stride=ZROWS), :] = part[:, 128 * n2 : 128 * n2 + 128]
    for n in range(4, 8):
        wide[pl.ds(2 * NPLANE + n, NZ, stride=ZROWS), :] = jnp.zeros((NZ, 128), F32)
    o_ref[...] = wide[...].astype(BF16)


def inward_kernel(r_ref, o_ref, before, after):
    before[...] = r_ref[...].astype(F32)
    for j in range(NPLANE):
        for a in range(2):
            after[pl.ds(PROWS * j + a, NZ, stride=2), :] = before[pl.ds(2 * j + a, NZ, stride=ZROWS), :]
    for zl in range(NZL):
        parts = [before[pl.ds((zh * NZL + zl) * ZROWS + 2 * NPLANE, 4), :] for zh in range(NZH)]
        block = jnp.concatenate(parts, axis=0)
        for y in range(NY):
            after[pl.ds((zl * NY + y) * PROWS + 2 * NZ, 8), :] = block
    o_ref[...] = after[...].astype(BF16)


def outward_kernel(y_ref, r_ref, o_ref, before, after):
    before[...] = r_ref[...].astype(F32)
    for j in range(NPLANE):
        for a in range(2):
            after[pl.ds(2 * j + a, NZ, stride=ZROWS), :] = before[pl.ds(PROWS * j + a, NZ, stride=2), :]
    for zl in range(NZL):
        at = pl.multiple_of((zl * NY + y_ref[0]) * PROWS + 2 * NZ, 8)
        block = before[pl.ds(at, 8), :]
        after[pl.ds(zl * ZROWS + 2 * NPLANE, 8), :] = block
        after[pl.ds((NZL + zl) * ZROWS + 2 * NPLANE, 8), :] = pltpu.roll(block, 4, 0)
    o_ref[...] = after[...].astype(BF16)


def unpack_kernel(r_ref, k_ref, v_ref, g_ref, gq_ref, gk_ref, gv_ref, gh_ref, tile, wide):
    blocks = k_ref.shape[1] // 128
    wide[...] = r_ref[...].astype(F32)
    for a in range(2):
        for half in range(2):
            planes = [
                wide[pl.ds((half * TOK + i) * ZROWS + a, blocks // 2, stride=2), :] for i in range(TOK)
            ]
            for t, plane in enumerate(swap_segments(planes)):
                tile[a, pl.ds(half * TOK + t, blocks // 2, stride=2 * TOK), :] = plane
    for block in range(blocks):
        lanes = pl.ds(block * 128, 128)
        conv = tile[0, pl.ds(block * TOK, TOK), :]
        corr = tile[1, pl.ds(block * TOK, TOK), :]
        gq_ref[:, lanes] = (g_ref[:, lanes].astype(F32) * conv).astype(BF16)
        gk_ref[:, lanes] = (corr * v_ref[:, lanes].astype(F32)).astype(BF16)
        gv_ref[:, lanes] = (corr * k_ref[:, lanes].astype(F32)).astype(BF16)
    order = phase_order(gh_ref.shape[1], True)
    total = None
    for n in range(2):
        rows = [wide[pl.ds(2 * NPLANE + 2 * n + n2, NZ, stride=ZROWS), :] for n2 in range(2)]
        part = jnp.dot(jnp.concatenate(rows, axis=1).astype(BF16), order, preferred_element_type=F32)
        total = part if total is None else total + part
    gh_ref[...] = total


def columns(x):
    return jnp.concatenate([x[b : b + 128].T for b in range(0, x.shape[0], 128)], axis=1)


def row_pieces():
    for x in range(NX):
        for zh in range(NZH):
            for core in range(NCORE):
                for y in range(NY):
                    q = (((x * NZH + zh) * NCORE + core) * NZL) * NY + y
                    sent = ((x * NCORE + core) * NY + y) * PROWS + 2 * NZL * zh
                    yield q, sent


def read_taps(y, wide):
    shape = (TOK, 128)
    row, seg = row_of(shape), lane_of(shape) // 32
    out = []
    for x in range(NX):
        column = jnp.zeros(shape, F32)
        for core in range(NCORE):
            at = pl.multiple_of(((x * NCORE + core) * NY + y) * PROWS + 2 * NZ, 8)
            got = wide[pl.ds(at, 8), :]
            for zh in range(NZH):
                low, high = (got[4 * zh + n : 4 * zh + n + 1] + got[4 * zh + n + 2 : 4 * zh + n + 3] for n in range(2))
                both = jnp.where(row < 4, low, high)
                place = zh * NCORE + core
                for d in range(4):
                    moved = pltpu.roll(both, 32 * ((place - d) % 4), 1) if place != d else both
                    column = jnp.where((seg == place) & (row % 4 == d), moved, column)
        out.append(column)
    return jnp.concatenate(out, axis=1)


def write_lags(lags, wide):
    shape = (TOK, 128)
    row, seg = row_of(shape), lane_of(shape) // 32
    for x in range(NX):
        column = lags[:, x * 128 : x * 128 + 128]
        for core in range(NCORE):
            rows = []
            for zh in range(NZH):
                place = zh * NCORE + core
                spread = jnp.zeros(shape, F32)
                for d in range(4):
                    moved = pltpu.roll(column, 32 * ((d - place) % 4), 1) if place != d else column
                    spread = jnp.where((seg == d) & (row % 4 == d), moved, spread)
                pair = [jnp.sum(spread[4 * n : 4 * n + 4], axis=0, keepdims=True) for n in range(2)]
                high = [value.astype(BF16).astype(F32) for value in pair]
                rows += high + [value - h for value, h in zip(pair, high)]
            block = jnp.concatenate(rows, axis=0)
            for y in range(NY):
                wide[pl.ds(((x * NCORE + core) * NY + y) * PROWS + 2 * NZ, 8), :] = block


def group_kernel(y_ref, r_ref, o_ref, wide, rows, lhs, ahead, base, hi, lo, flipped):
    count = rows.shape[1]
    nblk = count // ROWS
    lane8, row8 = lane_of((TOK, count)), row_of((TOK, count))
    wide[...] = r_ref[...].astype(F32)
    taps = read_taps(y_ref[0], wide)
    for p in range(TOK):
        skew = jnp.broadcast_to(taps[p : p + 1], (TOK, count))
        for bit in range(3):
            skew = jnp.where((row8 >> bit) & 1 == 1, pltpu.roll(skew, 1 << bit, 1), skew)
        for r in range(ROWS // 8):
            part = pltpu.roll(skew, 8 * r, 1) if r else skew
            base[pl.ds(8 * r, 8), :] = jnp.where(lane8 >= row8 + 8 * r, part, 0.0)
        whole = base[...]
        hi[pl.ds(p * ROWS, ROWS), :], lo[pl.ds(p * ROWS, ROWS), :] = halves(whole)
        for m in range(nblk):
            at = pl.ds(p * count + m * 128, 128)
            flipped[at, pl.ds(0, 128)], flipped[at, pl.ds(128, 128)] = halves(whole[:, m * 128 : (m + 1) * 128].T)
    for q, sent in row_pieces():
        for a in range(2):
            rows[a, pl.ds(q, NZL, stride=NY), :] = wide[pl.ds(sent + a, NZL, stride=2), :]
    sig, ups = rows[0], rows[1]
    sig_t, ups_t = columns(sig), columns(ups)
    lane = lane_of(sig_t.shape)
    sig_prev = jnp.where(lane == 0, 0.0, pltpu.roll(sig_t, 1, 1)).astype(BF16)
    ups_next = jnp.where(lane == count - 1, 0.0, pltpu.roll(ups_t, count - 1, 1)).astype(BF16)
    sig_t, ups_t = sig_t.astype(BF16), ups_t.astype(BF16)
    for p in range(TOK):
        cut = CH * p
        for b in range(nblk):
            cols = slice(b * 128, b * 128 + 128)
            if p:
                lhs[pl.ds(b * 128, cut), pl.ds(p * 128, 128)] = sig_prev[128 - cut :, cols]
            lhs[pl.ds(b * 128 + cut, 128 - cut), pl.ds(p * 128, 128)] = sig_t[: 128 - cut, cols]
            size = count - 128 * b
            ahead[pl.ds(b * 128, 128 - cut), pl.ds(p * count, size)] = ups_t[cut:, b * 128 :]
            if p:
                ahead[pl.ds(b * 128 + 128 - cut, cut), pl.ds(p * count, size)] = ups_next[:cut, b * 128 :]
            if b:
                ahead[pl.ds(b * 128, 128), pl.ds(p * count + size, 128 * b)] = jnp.zeros((128, 128 * b), BF16)
    side = jnp.concatenate([sig[b * 128 : b * 128 + 128] for b in range(nblk)], axis=1).astype(BF16)
    sums = []
    for p in range(TOK):
        lags = jnp.dot(side, ahead[:, pl.ds(p * count, count)], preferred_element_type=F32)
        total = jnp.zeros((TOK, count), F32)
        for r in range(ROWS // 8):
            part = jnp.where(lane8 >= row8 + 8 * r, lags[8 * r : 8 * r + 8], 0.0)
            total = total + (pltpu.roll(part, count - 8 * r, 1) if r else part)
        for bit in range(3):
            total = jnp.where((row8 >> bit) & 1 == 1, pltpu.roll(total, count - (1 << bit), 1), total)
        sums.append(jnp.sum(total, axis=0, keepdims=True))
    write_lags(jnp.concatenate(sums, axis=0), wide)
    conv = [None] * nblk
    for b in range(nblk):
        block = lhs[pl.ds(b * 128, 128), :]
        size = count - 128 * b
        part = jnp.dot(block, hi[:, pl.ds(0, size)], preferred_element_type=F32)
        part = part + jnp.dot(block, lo[:, pl.ds(0, size)], preferred_element_type=F32)
        for k in range(nblk - b):
            piece = part[:, k * 128 : k * 128 + 128]
            conv[b + k] = piece if conv[b + k] is None else conv[b + k] + piece
    back = jnp.dot(ahead[...], flipped[...], preferred_element_type=F32)
    for b in range(nblk):
        at = pl.ds(b * 128, 128)
        rows[0, at, :] = conv[b].T
        rows[1, at, :] = (back[b * 128 : b * 128 + 128, :128] + back[b * 128 : b * 128 + 128, 128:]).T
    for q, sent in row_pieces():
        for a in range(2):
            wide[pl.ds(sent + a, NZL, stride=2), :] = rows[a, pl.ds(q, NZL, stride=NY), :]
    o_ref[...] = wide[...].astype(BF16)


def params(mib):
    return pltpu.CompilerParams(vmem_limit_bytes=mib << 20)


def pack(query, key, value, grad, filters):
    rows = query.shape[1] // CH
    return pl.pallas_call(
        pack_kernel,
        out_shape=jax.ShapeDtypeStruct((NZ * ZROWS, 128), BF16),
        scratch_shapes=[pltpu.VMEM((2, rows, 128), F32), pltpu.VMEM((NZ * ZROWS, 128), F32)],
        compiler_params=params(8),
        name="pack",
    )(query, key, value, grad, filters)


def unpack(received, key, value, grad, filters):
    shape = jax.ShapeDtypeStruct(key.shape, BF16)
    rows = key.shape[1] // CH
    return pl.pallas_call(
        unpack_kernel,
        out_shape=(shape, shape, shape, jax.ShapeDtypeStruct(filters.shape, F32)),
        scratch_shapes=[pltpu.VMEM((2, rows, 128), F32), pltpu.VMEM((NZ * ZROWS, 128), F32)],
        compiler_params=params(8),
        name="unpack",
    )(received, key, value, grad)


def inward(received):
    return pl.pallas_call(
        inward_kernel,
        out_shape=jax.ShapeDtypeStruct((NPLANE * PROWS, 128), BF16),
        scratch_shapes=[pltpu.VMEM((NZ * ZROWS, 128), F32), pltpu.VMEM((NPLANE * PROWS, 128), F32)],
        compiler_params=params(8),
        name="inward",
    )(received)


def outward(y, received):
    return pl.pallas_call(
        outward_kernel,
        out_shape=jax.ShapeDtypeStruct((NZ * ZROWS, 128), BF16),
        in_specs=[pl.BlockSpec(memory_space=pltpu.SMEM), pl.BlockSpec(memory_space=pltpu.VMEM)],
        scratch_shapes=[pltpu.VMEM((NPLANE * PROWS, 128), F32), pltpu.VMEM((NZ * ZROWS, 128), F32)],
        compiler_params=params(8),
        name="outward",
    )(y, received)


def group(y, received):
    count = NZ * NPLANE
    return pl.pallas_call(
        group_kernel,
        out_shape=jax.ShapeDtypeStruct(received.shape, BF16),
        in_specs=[pl.BlockSpec(memory_space=pltpu.SMEM), pl.BlockSpec(memory_space=pltpu.VMEM)],
        scratch_shapes=[
            pltpu.VMEM(received.shape, F32),
            pltpu.VMEM((2, count, 128), F32),
            pltpu.VMEM((count, TOK * ROWS), BF16),
            pltpu.VMEM((count, TOK * count), BF16),
            pltpu.VMEM((ROWS, count), F32),
            pltpu.VMEM((TOK * ROWS, count), BF16),
            pltpu.VMEM((TOK * ROWS, count), BF16),
            pltpu.VMEM((TOK * count, 2 * ROWS), BF16),
        ],
        compiler_params=params(32),
        name="group",
    )(y, received)


def exchange(rows, axes, parts):
    chunks = rows.reshape(parts, rows.shape[0] // parts, 128)
    return lax.all_to_all(chunks, axes, 0, 0, tiled=True).reshape(rows.shape)


def on_device(query_gate, key_gate, value_proj, grad_out, long_filters):
    y = lax.axis_index("y").astype(jnp.int32).reshape(1)
    rows = pack(query_gate, key_gate, value_proj, grad_out, long_filters)
    rows = inward(exchange(rows, Z_AXES, NZ))
    rows = group(y, exchange(rows, PLANE_AXES, NPLANE))
    rows = outward(y, exchange(rows, PLANE_AXES, NPLANE))
    return unpack(exchange(rows, Z_AXES, NZ), key_gate, value_proj, grad_out, long_filters)


def solution(mesh):
    fine = Mesh(mesh.devices.reshape(NX, NZH, NCORE, NZL, NY), ("x", "zh", "core", "zl", "y"))
    tokens = P(("x", "zh", "core", "zl", "y"), None)
    filters = P(("zl", "y"), ("x", "zh", "core"))
    return jax.shard_map(
        on_device,
        mesh=fine,
        in_specs=(tokens, tokens, tokens, tokens, filters),
        out_specs=(tokens, tokens, tokens, filters),
        check_vma=False,
    )
```

time: 152 us -> 104 us (0.68)
  the two profiles are of different devices: /device:TPU:1 before, /device:TPU:8 now
where the time goes in v2:
time: 104 us
  blocking collectives  75.1 us (72%)
  Pallas kernels  8.21 us (8%)
  waiting for transfers between devices  7.7 us (7%)
  starting transfers between devices  7.53 us (7%)
  local copies, waits for them, and re-layouts  4.35 us (4%)
    all_to_all x3, blocking collectives, exchange(): return lax.all_to_all(chunks, axes, 0, 0, tiled=True).reshape(rows.shape)  75.1 us
    all_to_all x1, waiting for transfers between devices, exchange(): return lax.all_to_all(chunks, axes, 0, 0, tiled=True).reshape(rows.shape)  7.7 us
    all_to_all x1, starting transfers between devices, exchange(): return lax.all_to_all(chunks, axes, 0, 0, tiled=True).reshape(rows.shape)  7.53 us
    pallas_call x1, Pallas kernels, group(): pl.pallas_call(group_kernel, out_shape=jax.ShapeDtypeStruct(received.shap...  4.92 us
    unnamed x16, local copies, waits for them, and re-layouts  4.35 us
  transfers between devices with their start and end apart: 1, of which 1 were waited for; matrix products, arithmetic and copies ran while one was open for 0% of the time, Pallas kernels for 0%

profile of v2, /device:TPU:8, one launch (start us, length us, event | category | flops | bytes accessed | tf_op | source)
XLA Modules:
  0.0 103.6 jit_solution(14944627901841369539)
XLA Ops:
  0.6 0.0 copy-start
  0.6 0.9 copy-done
  1.5 0.0 copy-start.2
  1.5 0.9 copy-done.2
  2.4 0.0 copy-start.4
  2.4 0.9 copy-done.4
  3.3 0.0 copy-start.6
  3.3 0.9 copy-done.6
  4.3 0.0 copy-start.7
  4.3 0.7 copy-done.7
  5.0 0.8 pack.1
  5.8 34.4 %all_to_all.20 = bf16[16,72,128]{2,1,0:T(8,128)(2,1)S(1)} all-to-all(bf16[16,72,128]{2,1,0:T(8,128)(2,1)S(1)} %bitcast.12), channel_id=1, replica_groups=mesh['x'=4,'zh'=2,'core'=2,'zl'=8,'y'=4] {'zh','zl'}, dimensions={0} | all-to-all | bytes 589824 | tf_op jit(solution)/shard_map/all_to_all | solution.py:331
  40.2 0.9 inward.1
  41.1 7.5 %all-to-all-start.1 = ((bf16[32,40,128]{2,1,0:T(8,128)(2,1)}), bf16[32,40,128]{2,1,0:T(8,128)(2,1)S(1)}, u32[]{:S(2)}, u32[]{:S(2)}) async-start(bf16[32,40,128]{2,1,0:T(8,128)(2,1)} %bitcast.3), calls=%async_computation.1 | async-start | bytes 655360 | tf_op jit(solution)/shard_map/all_to_all | solution.py:331
  48.6 7.7 %all-to-all-done.1 = bf16[32,40,128]{2,1,0:T(8,128)(2,1)S(1)} async-done(((bf16[32,40,128]{2,1,0:T(8,128)(2,1)}), bf16[32,40,128]{2,1,0:T(8,128)(2,1)S(1)}, u32[]{:S(2)}, u32[]{:S(2)}) %all-to-all-start.1) | async-done | bytes 327712 | tf_op jit(solution)/shard_map/all_to_all | solution.py:331
  56.3 4.9 %group.1 = bf16[1280,128]{1,0:T(8,128)(2,1)S(1)} custom-call(s32[1]{0:T(128)} %bitcast.y_ref, bf16[1280,128]{1,0:T(8,128)(2,1)S(1)} %bitcast.9), custom_call_target="tpu_custom_call" | custom-call | tf_op jit(solution)/shard_map/group/pallas_call | solution.py:310
  61.2 13.4 %all_to_all.21 = bf16[32,40,128]{2,1,0:T(8,128)(2,1)S(1)} all-to-all(bf16[32,40,128]{2,1,0:T(8,128)(2,1)S(1)} %bitcast.11), channel_id=1, replica_groups=mesh['x'=4,'zh'=2,'core'=2,'zl'=8,'y'=4] {'x','core','y'}, dimensions={0} | all-to-all | bytes 655360 | tf_op jit(solution)/shard_map/all_to_all | solution.py:331
  74.6 0.2 outward.1
  74.8 0.0 copy-start.1
  74.8 0.0 copy-start.3
  74.8 0.0 copy-start.5
  74.8 27.3 %all_to_all.22 = bf16[16,72,128]{2,1,0:T(8,128)(2,1)S(1)} all-to-all(bf16[16,72,128]{2,1,0:T(8,128)(2,1)S(1)} %bitcast.14), channel_id=1, replica_groups=mesh['x'=4,'zh'=2,'core'=2,'zl'=8,'y'=4] {'zh','zl'}, dimensions={0} | all-to-all | bytes 589824 | tf_op jit(solution)/shard_map/all_to_all | solution.py:331
  102.1 0.0 copy-done.1
  102.1 0.0 copy-done.3
  102.1 0.0 copy-done.5
  102.1 1.4 %unpack.1 = (bf16[8,8192]{1,0:T(8,128)(2,1)}, bf16[8,8192]{1,0:T(8,128)(2,1)}, bf16[8,8192]{1,0:T(8,128)(2,1)}, f32[16,256]{1,0:T(8,128)}) custom-call(bf16[1152,128]{1,0:T(8,128)(2,1)S(1)} %bitcast.15, bf16[8,8192]{1,0:T(8,128)(2,1)S(1)} %copy-done.1, bf16[8,8192]{1,0:T(8,128)(2,1)S(1)} %copy-done.3, bf16[8,8192]{1,0:T(8,128)(2,1)S(1)} %copy-done.5), custom_call_target="tpu_custom_call" | custom-call | tf_op jit(solution)/shard_map/unpack/pallas_call | solution.py:278
Async XLA Ops:
  0.6 0.9 copy-start
  1.5 0.9 copy-start.2
  2.4 0.9 copy-start.4
  3.3 0.9 copy-start.6
  4.3 0.7 copy-start.7
  41.1 15.2 %all-to-all-start.1 = ((bf16[32,40,128]{2,1,0:T(8,128)(2,1)}), bf16[32,40,128]{2,1,0:T(8,128)(2,1)S(1)}, u32[]{:S(2)}, u32[]{:S(2)}) async-start(bf16[32,40,128]{2,1,0:T(8,128)(2,1)} %bitcast.3), calls=%async_computation.1 | async-start | bytes 655360 | tf_op jit(solution)/shard_map/all_to_all | solution.py:331
  74.8 27.4 %copy-start.1 = (bf16[8,8192]{1,0:T(8,128)(2,1)S(1)}, bf16[8,8192]{1,0:T(8,128)(2,1)}, u32[]{:S(2)}) copy-start(bf16[8,8192]{1,0:T(8,128)(2,1)} %k_ref.3) | copy-start | bytes 393220
  74.8 27.3 %copy-start.3 = (bf16[8,8192]{1,0:T(8,128)(2,1)S(1)}, bf16[8,8192]{1,0:T(8,128)(2,1)}, u32[]{:S(2)}) copy-start(bf16[8,8192]{1,0:T(8,128)(2,1)} %v_ref.3) | copy-start | bytes 393220
  74.8 27.3 %copy-start.5 = (bf16[8,8192]{1,0:T(8,128)(2,1)S(1)}, bf16[8,8192]{1,0:T(8,128)(2,1)}, u32[]{:S(2)}) copy-start(bf16[8,8192]{1,0:T(8,128)(2,1)} %g_ref.3) | copy-start | bytes 393220

commit v3 on v2

--- a/solution.py
+++ b/solution.py
@@ -12,7 +12,7 @@
 NX, NZH, NCORE, NZL, NY = 4, 2, 2, 8, 4
 NZ = NZH * NZL
 NPLANE = NX * NCORE * NY
-ZROWS = 2 * NPLANE + 8
+ZROWS = 2 * NPLANE + 4
 PROWS = 2 * NZ + 8
 Z_AXES = ("zh", "zl")
 PLANE_AXES = ("x", "core", "y")
@@ -57,24 +57,31 @@
     return high, (x - high.astype(F32)).astype(BF16)
 
 
-def pack_kernel(q_ref, k_ref, v_ref, g_ref, h_ref, o_ref, tile, wide):
-    blocks = q_ref.shape[1] // 128
-    for a, (x_ref, y_ref) in enumerate(((k_ref, v_ref), (g_ref, q_ref))):
+def pack_kernel(k_hbm, v_hbm, g_hbm, q_hbm, h_hbm, o_ref, inputs, taps, tile, wide, sems):
+    copies = [
+        pltpu.make_async_copy(hbm, inputs.at[n], sems.at[n]) for n, hbm in enumerate((k_hbm, v_hbm, g_hbm, q_hbm))
+    ]
+    copies.append(pltpu.make_async_copy(h_hbm, taps, sems.at[4]))
+    for copy in copies[4:] + copies[:4]:
+        copy.start()
+    order = phase_order(taps.shape[1], False)
+    copies[4].wait()
+    for n, part in enumerate(halves(taps[...])):
+        part = jnp.dot(part, order, preferred_element_type=F32)
+        for n2 in range(2):
+            wide[pl.ds(2 * NPLANE + 2 * n + n2, NZ, stride=ZROWS), :] = part[:, 128 * n2 : 128 * n2 + 128]
+    blocks = k_hbm.shape[1] // 128
+    for a in range(2):
+        copies[2 * a].wait()
+        copies[2 * a + 1].wait()
         for block in range(blocks):
             lanes = pl.ds(block * 128, 128)
-            prod = (x_ref[:, lanes].astype(F32) * y_ref[:, lanes].astype(F32)).astype(BF16)
+            prod = (inputs[2 * a, :, lanes].astype(F32) * inputs[2 * a + 1, :, lanes].astype(F32)).astype(BF16)
             tile[a, pl.ds(block * TOK, TOK), :] = prod.astype(F32)
         for half in range(2):
             planes = [tile[a, pl.ds(half * TOK + t, blocks // 2, stride=2 * TOK), :] for t in range(TOK)]
             for i, plane in enumerate(swap_segments(planes)):
                 wide[pl.ds((half * TOK + i) * ZROWS + a, blocks // 2, stride=2), :] = plane
-    order = phase_order(h_ref.shape[1], False)
-    for n, part in enumerate(halves(h_ref[...])):
-        part = jnp.dot(part, order, preferred_element_type=F32)
-        for n2 in range(2):
-            wide[pl.ds(2 * NPLANE + 2 * n + n2, NZ, stride=ZROWS), :] = part[:, 128 * n2 : 128 * n2 + 128]
-    for n in range(4, 8):
-        wide[pl.ds(2 * NPLANE + n, NZ, stride=ZROWS), :] = jnp.zeros((NZ, 128), F32)
     o_ref[...] = wide[...].astype(BF16)
 
 
@@ -91,21 +98,25 @@
     o_ref[...] = after[...].astype(BF16)
 
 
-def outward_kernel(y_ref, r_ref, o_ref, before, after):
+def outward_kernel(r_ref, o_ref, before, after):
+    own = lax.axis_index("y")
     before[...] = r_ref[...].astype(F32)
     for j in range(NPLANE):
         for a in range(2):
             after[pl.ds(2 * j + a, NZ, stride=ZROWS), :] = before[pl.ds(PROWS * j + a, NZ, stride=2), :]
     for zl in range(NZL):
-        at = pl.multiple_of((zl * NY + y_ref[0]) * PROWS + 2 * NZ, 8)
+        at = pl.multiple_of((zl * NY + own) * PROWS + 2 * NZ, 8)
         block = before[pl.ds(at, 8), :]
-        after[pl.ds(zl * ZROWS + 2 * NPLANE, 8), :] = block
-        after[pl.ds((NZL + zl) * ZROWS + 2 * NPLANE, 8), :] = pltpu.roll(block, 4, 0)
+        for zh in range(NZH):
+            after[pl.ds((zh * NZL + zl) * ZROWS + 2 * NPLANE, 4), :] = block[4 * zh : 4 * zh + 4]
     o_ref[...] = after[...].astype(BF16)
 
 
-def unpack_kernel(r_ref, k_ref, v_ref, g_ref, gq_ref, gk_ref, gv_ref, gh_ref, tile, wide):
+def unpack_kernel(r_ref, k_ref, v_ref, g_ref, gq_hbm, gk_hbm, gv_hbm, gh_ref, results, tile, wide, sems):
     blocks = k_ref.shape[1] // 128
+    copies = [
+        pltpu.make_async_copy(results.at[n], hbm, sems.at[n]) for n, hbm in enumerate((gq_hbm, gk_hbm, gv_hbm))
+    ]
     wide[...] = r_ref[...].astype(F32)
     for a in range(2):
         for half in range(2):
@@ -114,13 +125,12 @@
             ]
             for t, plane in enumerate(swap_segments(planes)):
                 tile[a, pl.ds(half * TOK + t, blocks // 2, stride=2 * TOK), :] = plane
-    for block in range(blocks):
-        lanes = pl.ds(block * 128, 128)
-        conv = tile[0, pl.ds(block * TOK, TOK), :]
-        corr = tile[1, pl.ds(block * TOK, TOK), :]
-        gq_ref[:, lanes] = (g_ref[:, lanes].astype(F32) * conv).astype(BF16)
-        gk_ref[:, lanes] = (corr * v_ref[:, lanes].astype(F32)).astype(BF16)
-        gv_ref[:, lanes] = (corr * k_ref[:, lanes].astype(F32)).astype(BF16)
+        for n, gate in enumerate((v_ref, k_ref) if a else (g_ref,)):
+            for block in range(blocks):
+                lanes = pl.ds(block * 128, 128)
+                value = gate[:, lanes].astype(F32) * tile[a, pl.ds(block * TOK, TOK), :]
+                results[a + n, :, lanes] = value.astype(BF16)
+            copies[a + n].start()
     order = phase_order(gh_ref.shape[1], True)
     total = None
     for n in range(2):
@@ -128,6 +138,8 @@
         part = jnp.dot(jnp.concatenate(rows, axis=1).astype(BF16), order, preferred_element_type=F32)
         total = part if total is None else total + part
     gh_ref[...] = total
+    for copy in copies:
+        copy.wait()
 
 
 def columns(x):
@@ -185,12 +197,12 @@
                 wide[pl.ds(((x * NCORE + core) * NY + y) * PROWS + 2 * NZ, 8), :] = block
 
 
-def group_kernel(y_ref, r_ref, o_ref, wide, rows, lhs, ahead, base, hi, lo, flipped):
+def group_kernel(r_ref, o_ref, wide, rows, lhs, ahead, base, hi, lo, flipped):
     count = rows.shape[1]
     nblk = count // ROWS
     lane8, row8 = lane_of((TOK, count)), row_of((TOK, count))
     wide[...] = r_ref[...].astype(F32)
-    taps = read_taps(y_ref[0], wide)
+    taps = read_taps(lax.axis_index("y"), wide)
     for p in range(TOK):
         skew = jnp.broadcast_to(taps[p : p + 1], (TOK, count))
         for bit in range(3):
@@ -266,10 +278,17 @@
     return pl.pallas_call(
         pack_kernel,
         out_shape=jax.ShapeDtypeStruct((NZ * ZROWS, 128), BF16),
-        scratch_shapes=[pltpu.VMEM((2, rows, 128), F32), pltpu.VMEM((NZ * ZROWS, 128), F32)],
+        in_specs=[pl.BlockSpec(memory_space=pltpu.HBM)] * 5,
+        scratch_shapes=[
+            pltpu.VMEM((4, *query.shape), BF16),
+            pltpu.VMEM(filters.shape, F32),
+            pltpu.VMEM((2, rows, 128), F32),
+            pltpu.VMEM((NZ * ZROWS, 128), F32),
+            pltpu.SemaphoreType.DMA((5,)),
+        ],
         compiler_params=params(8),
         name="pack",
-    )(query, key, value, grad, filters)
+    )(*(pltpu.with_memory_space_constraint(x, pltpu.HBM) for x in (key, value, grad, query, filters)))
 
 
 def unpack(received, key, value, grad, filters):
@@ -278,7 +297,13 @@
     return pl.pallas_call(
         unpack_kernel,
         out_shape=(shape, shape, shape, jax.ShapeDtypeStruct(filters.shape, F32)),
-        scratch_shapes=[pltpu.VMEM((2, rows, 128), F32), pltpu.VMEM((NZ * ZROWS, 128), F32)],
+        out_specs=[pl.BlockSpec(memory_space=pltpu.HBM)] * 3 + [pl.BlockSpec(memory_space=pltpu.VMEM)],
+        scratch_shapes=[
+            pltpu.VMEM((3, *key.shape), BF16),
+            pltpu.VMEM((2, rows, 128), F32),
+            pltpu.VMEM((NZ * ZROWS, 128), F32),
+            pltpu.SemaphoreType.DMA((3,)),
+        ],
         compiler_params=params(8),
         name="unpack",
     )(received, key, value, grad)
@@ -294,23 +319,21 @@
     )(received)
 
 
-def outward(y, received):
+def outward(received):
     return pl.pallas_call(
         outward_kernel,
         out_shape=jax.ShapeDtypeStruct((NZ * ZROWS, 128), BF16),
-        in_specs=[pl.BlockSpec(memory_space=pltpu.SMEM), pl.BlockSpec(memory_space=pltpu.VMEM)],
         scratch_shapes=[pltpu.VMEM((NPLANE * PROWS, 128), F32), pltpu.VMEM((NZ * ZROWS, 128), F32)],
         compiler_params=params(8),
         name="outward",
-    )(y, received)
-
-
-def group(y, received):
+    )(received)
+
+
+def group(received):
     count = NZ * NPLANE
     return pl.pallas_call(
         group_kernel,
         out_shape=jax.ShapeDtypeStruct(received.shape, BF16),
-        in_specs=[pl.BlockSpec(memory_space=pltpu.SMEM), pl.BlockSpec(memory_space=pltpu.VMEM)],
         scratch_shapes=[
             pltpu.VMEM(received.shape, F32),
             pltpu.VMEM((2, count, 128), F32),
@@ -323,21 +346,20 @@
         ],
         compiler_params=params(32),
         name="group",
-    )(y, received)
-
-
-def exchange(rows, axes, parts):
-    chunks = rows.reshape(parts, rows.shape[0] // parts, 128)
+    )(received)
+
+
+def exchange(rows, axes):
+    chunks = rows.reshape(-1, 4, 128)
     return lax.all_to_all(chunks, axes, 0, 0, tiled=True).reshape(rows.shape)
 
 
 def on_device(query_gate, key_gate, value_proj, grad_out, long_filters):
-    y = lax.axis_index("y").astype(jnp.int32).reshape(1)
     rows = pack(query_gate, key_gate, value_proj, grad_out, long_filters)
-    rows = inward(exchange(rows, Z_AXES, NZ))
-    rows = group(y, exchange(rows, PLANE_AXES, NPLANE))
-    rows = outward(y, exchange(rows, PLANE_AXES, NPLANE))
-    return unpack(exchange(rows, Z_AXES, NZ), key_gate, value_proj, grad_out, long_filters)
+    rows = inward(exchange(rows, Z_AXES))
+    rows = group(exchange(rows, PLANE_AXES))
+    rows = outward(exchange(rows, PLANE_AXES))
+    return unpack(exchange(rows, Z_AXES), key_gate, value_proj, grad_out, long_filters)
 
 
 def solution(mesh):

time: 104 us -> 99.1 us (0.953)
  blocking collectives: 75.1 us -> 88.8 us
  waiting for transfers between devices: 7.7 us -> 0 us
  starting transfers between devices: 7.53 us -> 0 us
  local copies, waits for them, and re-layouts: 4.35 us -> 0.02 us
    all_to_all x3 -> x4, blocking collectives: 75.1 us -> 88.8 us  [exchange(): return lax.all_to_all(chunks, axes, 0, 0, tiled=True).reshape(rows.shape)]
    all_to_all x1 -> x0, waiting for transfers between devices: 7.7 us -> none  [exchange(): return lax.all_to_all(chunks, axes, 0, 0, tiled=True).reshape(rows.shape)]
    all_to_all x1 -> x0, starting transfers between devices: 7.53 us -> none  [exchange(): return lax.all_to_all(chunks, axes, 0, 0, tiled=True).reshape(rows.shape)]
    unnamed x16 -> x6, local copies, waits for them, and re-layouts: 4.35 us -> 0.02 us
    pallas_call x1, Pallas kernels: 0.84 us -> 1.92 us  [pack(): pl.pallas_call(pack_kernel, out_shape=jax.ShapeDtypeStruct((NZ * ZROWS, 1...]
  transfers between devices with their start and end apart: 1 -> 0, of which waited for: 1 -> 0; matrix products, arithmetic and copies ran while one was open for 0% -> 0% of each run, Pallas kernels for 0% -> 0%
where the time goes in v3:
time: 99.1 us; the launch traced here: 98.7 us
  blocking collectives  88.8 us (90%)
  Pallas kernels  9.16 us (9%)
    all_to_all x4, blocking collectives, exchange(): return lax.all_to_all(chunks, axes, 0, 0, tiled=True).reshape(rows.shape)  88.8 us
    pallas_call x1, Pallas kernels, group(): pl.pallas_call(group_kernel, out_shape=jax.ShapeDtypeStruct(received.shap...  4.97 us
    pallas_call x1, Pallas kernels, unpack(): pl.pallas_call(unpack_kernel, out_shape=(shape, shape, shape, jax.ShapeDt...  2.04 us

profile of v3, /device:TPU:8, one launch (start us, length us, event | category | flops | bytes accessed | tf_op | source)
XLA Modules:
  0.0 98.7 jit_solution(2336976790065691096)
XLA Ops:
  0.6 1.9 %pack.1 = bf16[1088,128]{1,0:T(8,128)(2,1)S(1)} custom-call(bf16[8,8192]{1,0:T(8,128)(2,1)} %k_ref.1, bf16[8,8192]{1,0:T(8,128)(2,1)} %v_ref.1, bf16[8,8192]{1,0:T(8,128)(2,1)} %g_ref.1, bf16[8,8192]{1,0:T(8,128)(2,1)} %q_hbm.1, f32[16,256]{1,0:T(8,128)} %h_hbm.1), custom_call_target="tpu_custom_call" | custom-call | tf_op jit(solution)/shard_map/pack/pallas_call | solution.py:278
  2.6 33.9 %all_to_all.20 = bf16[272,4,128]{2,1,0:T(4,128)(2,1)S(1)} all-to-all(bf16[272,4,128]{2,1,0:T(4,128)(2,1)S(1)} %bitcast.15), channel_id=1, replica_groups=mesh['x'=4,'zh'=2,'core'=2,'zl'=8,'y'=4] {'zh','zl'}, dimensions={0} | all-to-all | bytes 557056 | tf_op jit(solution)/shard_map/all_to_all | solution.py:354
  36.5 0.1 inward.1
  36.6 15.0 %all_to_all.21 = bf16[320,4,128]{2,1,0:T(4,128)(2,1)S(1)} all-to-all(bf16[320,4,128]{2,1,0:T(4,128)(2,1)S(1)} %bitcast.8), channel_id=1, replica_groups=mesh['x'=4,'zh'=2,'core'=2,'zl'=8,'y'=4] {'x','core','y'}, dimensions={0} | all-to-all | bytes 655360 | tf_op jit(solution)/shard_map/all_to_all | solution.py:354
  51.6 5.0 %group.1 = bf16[1280,128]{1,0:T(8,128)(2,1)S(1)} custom-call(bf16[1280,128]{1,0:T(8,128)(2,1)S(1)} %bitcast.9), custom_call_target="tpu_custom_call" | custom-call | tf_op jit(solution)/shard_map/group/pallas_call | solution.py:334
  56.6 13.4 %all_to_all.22 = bf16[320,4,128]{2,1,0:T(4,128)(2,1)S(1)} all-to-all(bf16[320,4,128]{2,1,0:T(4,128)(2,1)S(1)} %bitcast.10), channel_id=1, replica_groups=mesh['x'=4,'zh'=2,'core'=2,'zl'=8,'y'=4] {'x','core','y'}, dimensions={0} | all-to-all | bytes 655360 | tf_op jit(solution)/shard_map/all_to_all | solution.py:354
  70.0 0.1 outward.1
  70.1 0.0 copy-start
  70.1 0.0 copy-start.1
  70.1 0.0 copy-start.2
  70.1 26.5 %all_to_all.23 = bf16[272,4,128]{2,1,0:T(4,128)(2,1)S(1)} all-to-all(bf16[272,4,128]{2,1,0:T(4,128)(2,1)S(1)} %bitcast.14), channel_id=1, replica_groups=mesh['x'=4,'zh'=2,'core'=2,'zl'=8,'y'=4] {'zh','zl'}, dimensions={0} | all-to-all | bytes 557056 | tf_op jit(solution)/shard_map/all_to_all | solution.py:354
  96.6 0.0 copy-done
  96.6 0.0 copy-done.1
  96.6 0.0 copy-done.2
  96.7 2.0 %unpack.1 = (bf16[8,8192]{1,0:T(8,128)(2,1)}, bf16[8,8192]{1,0:T(8,128)(2,1)}, bf16[8,8192]{1,0:T(8,128)(2,1)}, f32[16,256]{1,0:T(8,128)}) custom-call(bf16[1088,128]{1,0:T(8,128)(2,1)S(1)} %bitcast.12, bf16[8,8192]{1,0:T(8,128)(2,1)S(1)} %copy-done, bf16[8,8192]{1,0:T(8,128)(2,1)S(1)} %copy-done.1, bf16[8,8192]{1,0:T(8,128)(2,1)S(1)} %copy-done.2), custom_call_target="tpu_custom_call" | custom-call | tf_op jit(solution)/shard_map/unpack/pallas_call | solution.py:297
Async XLA Ops:
  70.1 26.6 %copy-start = (bf16[8,8192]{1,0:T(8,128)(2,1)S(1)}, bf16[8,8192]{1,0:T(8,128)(2,1)}, u32[]{:S(2)}) copy-start(bf16[8,8192]{1,0:T(8,128)(2,1)} %k_ref.1) | copy-start | bytes 393220
  70.1 26.6 %copy-start.1 = (bf16[8,8192]{1,0:T(8,128)(2,1)S(1)}, bf16[8,8192]{1,0:T(8,128)(2,1)}, u32[]{:S(2)}) copy-start(bf16[8,8192]{1,0:T(8,128)(2,1)} %v_ref.1) | copy-start | bytes 393220
  70.1 26.6 %copy-start.2 = (bf16[8,8192]{1,0:T(8,128)(2,1)S(1)}, bf16[8,8192]{1,0:T(8,128)(2,1)}, u32[]{:S(2)}) copy-start(bf16[8,8192]{1,0:T(8,128)(2,1)} %g_ref.1) | copy-start | bytes 393220

commit v4 on v3

--- a/solution.py
+++ b/solution.py
@@ -112,11 +112,8 @@
     o_ref[...] = after[...].astype(BF16)
 
 
-def unpack_kernel(r_ref, k_ref, v_ref, g_ref, gq_hbm, gk_hbm, gv_hbm, gh_ref, results, tile, wide, sems):
+def unpack_kernel(r_ref, k_ref, v_ref, g_ref, gq_ref, gk_ref, gv_ref, gh_ref, tile, wide):
     blocks = k_ref.shape[1] // 128
-    copies = [
-        pltpu.make_async_copy(results.at[n], hbm, sems.at[n]) for n, hbm in enumerate((gq_hbm, gk_hbm, gv_hbm))
-    ]
     wide[...] = r_ref[...].astype(F32)
     for a in range(2):
         for half in range(2):
@@ -125,12 +122,13 @@
             ]
             for t, plane in enumerate(swap_segments(planes)):
                 tile[a, pl.ds(half * TOK + t, blocks // 2, stride=2 * TOK), :] = plane
-        for n, gate in enumerate((v_ref, k_ref) if a else (g_ref,)):
-            for block in range(blocks):
-                lanes = pl.ds(block * 128, 128)
-                value = gate[:, lanes].astype(F32) * tile[a, pl.ds(block * TOK, TOK), :]
-                results[a + n, :, lanes] = value.astype(BF16)
-            copies[a + n].start()
+    for block in range(blocks):
+        lanes = pl.ds(block * 128, 128)
+        conv = tile[0, pl.ds(block * TOK, TOK), :]
+        corr = tile[1, pl.ds(block * TOK, TOK), :]
+        gq_ref[:, lanes] = (g_ref[:, lanes].astype(F32) * conv).astype(BF16)
+        gk_ref[:, lanes] = (corr * v_ref[:, lanes].astype(F32)).astype(BF16)
+        gv_ref[:, lanes] = (corr * k_ref[:, lanes].astype(F32)).astype(BF16)
     order = phase_order(gh_ref.shape[1], True)
     total = None
     for n in range(2):
@@ -138,8 +136,6 @@
         part = jnp.dot(jnp.concatenate(rows, axis=1).astype(BF16), order, preferred_element_type=F32)
         total = part if total is None else total + part
     gh_ref[...] = total
-    for copy in copies:
-        copy.wait()
 
 
 def columns(x):
@@ -197,7 +193,7 @@
                 wide[pl.ds(((x * NCORE + core) * NY + y) * PROWS + 2 * NZ, 8), :] = block
 
 
-def group_kernel(r_ref, o_ref, wide, rows, lhs, ahead, base, hi, lo, flipped):
+def group_kernel(r_ref, o_ref, wide, rows, lhs, ahead, hi, lo, flipped):
     count = rows.shape[1]
     nblk = count // ROWS
     lane8, row8 = lane_of((TOK, count)), row_of((TOK, count))
@@ -207,14 +203,14 @@
         skew = jnp.broadcast_to(taps[p : p + 1], (TOK, count))
         for bit in range(3):
             skew = jnp.where((row8 >> bit) & 1 == 1, pltpu.roll(skew, 1 << bit, 1), skew)
-        for r in range(ROWS // 8):
-            part = pltpu.roll(skew, 8 * r, 1) if r else skew
-            base[pl.ds(8 * r, 8), :] = jnp.where(lane8 >= row8 + 8 * r, part, 0.0)
-        whole = base[...]
-        hi[pl.ds(p * ROWS, ROWS), :], lo[pl.ds(p * ROWS, ROWS), :] = halves(whole)
-        for m in range(nblk):
-            at = pl.ds(p * count + m * 128, 128)
-            flipped[at, pl.ds(0, 128)], flipped[at, pl.ds(128, 128)] = halves(whole[:, m * 128 : (m + 1) * 128].T)
+        for r in range(0, ROWS // 8, 2):
+            pair = [
+                jnp.where(lane8 >= row8 + 8 * n, pltpu.roll(skew, 8 * n, 1) if n else skew, 0.0) for n in (r, r + 1)
+            ]
+            high, low = halves(jnp.concatenate(pair, axis=0))
+            hi[pl.ds(p * ROWS + 8 * r, 16), :], lo[pl.ds(p * ROWS + 8 * r, 16), :] = high, low
+            flipped[pl.ds(8 * r, 16), pl.ds(p * count, count)] = high
+            flipped[pl.ds(ROWS + 8 * r, 16), pl.ds(p * count, count)] = low
     for q, sent in row_pieces():
         for a in range(2):
             rows[a, pl.ds(q, NZL, stride=NY), :] = wide[pl.ds(sent + a, NZL, stride=2), :]
@@ -258,7 +254,7 @@
         for k in range(nblk - b):
             piece = part[:, k * 128 : k * 128 + 128]
             conv[b + k] = piece if conv[b + k] is None else conv[b + k] + piece
-    back = jnp.dot(ahead[...], flipped[...], preferred_element_type=F32)
+    back = lax.dot_general(ahead[...], flipped[...], (((1,), (1,)), ((), ())), preferred_element_type=F32)
     for b in range(nblk):
         at = pl.ds(b * 128, 128)
         rows[0, at, :] = conv[b].T
@@ -297,13 +293,7 @@
     return pl.pallas_call(
         unpack_kernel,
         out_shape=(shape, shape, shape, jax.ShapeDtypeStruct(filters.shape, F32)),
-        out_specs=[pl.BlockSpec(memory_space=pltpu.HBM)] * 3 + [pl.BlockSpec(memory_space=pltpu.VMEM)],
-        scratch_shapes=[
-            pltpu.VMEM((3, *key.shape), BF16),
-            pltpu.VMEM((2, rows, 128), F32),
-            pltpu.VMEM((NZ * ZROWS, 128), F32),
-            pltpu.SemaphoreType.DMA((3,)),
-        ],
+        scratch_shapes=[pltpu.VMEM((2, rows, 128), F32), pltpu.VMEM((NZ * ZROWS, 128), F32)],
         compiler_params=params(8),
         name="unpack",
     )(received, key, value, grad)
@@ -339,10 +329,9 @@
             pltpu.VMEM((2, count, 128), F32),
             pltpu.VMEM((count, TOK * ROWS), BF16),
             pltpu.VMEM((count, TOK * count), BF16),
-            pltpu.VMEM((ROWS, count), F32),
             pltpu.VMEM((TOK * ROWS, count), BF16),
             pltpu.VMEM((TOK * ROWS, count), BF16),
-            pltpu.VMEM((TOK * count, 2 * ROWS), BF16),
+            pltpu.VMEM((2 * ROWS, TOK * count), BF16),
         ],
         compiler_params=params(32),
         name="group",

time: 99.1 us -> 97.7 us (0.986)
  Pallas kernels: 9.16 us -> 7.79 us
where the time goes in v4:
time: 97.7 us; the launch traced here: 97.3 us
  blocking collectives  88.8 us (91%)
  Pallas kernels  7.79 us (8%)
    all_to_all x4, blocking collectives, exchange(): return lax.all_to_all(chunks, axes, 0, 0, tiled=True).reshape(rows.shape)  88.8 us
    pallas_call x1, Pallas kernels, group(): pl.pallas_call(group_kernel, out_shape=jax.ShapeDtypeStruct(received.shap...  4.23 us

profile of v4, /device:TPU:8, one launch (start us, length us, event | category | flops | bytes accessed | tf_op | source)
XLA Modules:
  0.0 97.3 jit_solution(14436042285326372059)
XLA Ops:
  0.6 1.9 %pack.1 = bf16[1088,128]{1,0:T(8,128)(2,1)S(1)} custom-call(bf16[8,8192]{1,0:T(8,128)(2,1)} %k_ref.1, bf16[8,8192]{1,0:T(8,128)(2,1)} %v_ref.1, bf16[8,8192]{1,0:T(8,128)(2,1)} %g_ref.1, bf16[8,8192]{1,0:T(8,128)(2,1)} %q_hbm.1, f32[16,256]{1,0:T(8,128)} %h_hbm.1), custom_call_target="tpu_custom_call" | custom-call | tf_op jit(solution)/shard_map/pack/pallas_call | solution.py:274
  2.6 33.9 %all_to_all.20 = bf16[272,4,128]{2,1,0:T(4,128)(2,1)S(1)} all-to-all(bf16[272,4,128]{2,1,0:T(4,128)(2,1)S(1)} %bitcast.15), channel_id=1, replica_groups=mesh['x'=4,'zh'=2,'core'=2,'zl'=8,'y'=4] {'zh','zl'}, dimensions={0} | all-to-all | bytes 557056 | tf_op jit(solution)/shard_map/all_to_all | solution.py:343
  36.5 0.1 inward.1
  36.6 15.0 %all_to_all.21 = bf16[320,4,128]{2,1,0:T(4,128)(2,1)S(1)} all-to-all(bf16[320,4,128]{2,1,0:T(4,128)(2,1)S(1)} %bitcast.8), channel_id=1, replica_groups=mesh['x'=4,'zh'=2,'core'=2,'zl'=8,'y'=4] {'x','core','y'}, dimensions={0} | all-to-all | bytes 655360 | tf_op jit(solution)/shard_map/all_to_all | solution.py:343
  51.6 4.2 %group.1 = bf16[1280,128]{1,0:T(8,128)(2,1)S(1)} custom-call(bf16[1280,128]{1,0:T(8,128)(2,1)S(1)} %bitcast.9), custom_call_target="tpu_custom_call" | custom-call | tf_op jit(solution)/shard_map/group/pallas_call | solution.py:324
  55.9 13.4 %all_to_all.22 = bf16[320,4,128]{2,1,0:T(4,128)(2,1)S(1)} all-to-all(bf16[320,4,128]{2,1,0:T(4,128)(2,1)S(1)} %bitcast.10), channel_id=1, replica_groups=mesh['x'=4,'zh'=2,'core'=2,'zl'=8,'y'=4] {'x','core','y'}, dimensions={0} | all-to-all | bytes 655360 | tf_op jit(solution)/shard_map/all_to_all | solution.py:343
  69.2 0.1 outward.1
  69.3 0.0 copy-start
  69.3 0.0 copy-start.1
  69.3 0.0 copy-start.2
  69.4 26.5 %all_to_all.23 = bf16[272,4,128]{2,1,0:T(4,128)(2,1)S(1)} all-to-all(bf16[272,4,128]{2,1,0:T(4,128)(2,1)S(1)} %bitcast.14), channel_id=1, replica_groups=mesh['x'=4,'zh'=2,'core'=2,'zl'=8,'y'=4] {'zh','zl'}, dimensions={0} | all-to-all | bytes 557056 | tf_op jit(solution)/shard_map/all_to_all | solution.py:343
  95.9 0.0 copy-done
  95.9 0.0 copy-done.1
  95.9 0.0 copy-done.2
  95.9 1.4 %unpack.1 = (bf16[8,8192]{1,0:T(8,128)(2,1)}, bf16[8,8192]{1,0:T(8,128)(2,1)}, bf16[8,8192]{1,0:T(8,128)(2,1)}, f32[16,256]{1,0:T(8,128)}) custom-call(bf16[1088,128]{1,0:T(8,128)(2,1)S(1)} %bitcast.12, bf16[8,8192]{1,0:T(8,128)(2,1)S(1)} %copy-done, bf16[8,8192]{1,0:T(8,128)(2,1)S(1)} %copy-done.1, bf16[8,8192]{1,0:T(8,128)(2,1)S(1)} %copy-done.2), custom_call_target="tpu_custom_call" | custom-call | tf_op jit(solution)/shard_map/unpack/pallas_call | solution.py:293
Async XLA Ops:
  69.3 26.6 %copy-start = (bf16[8,8192]{1,0:T(8,128)(2,1)S(1)}, bf16[8,8192]{1,0:T(8,128)(2,1)}, u32[]{:S(2)}) copy-start(bf16[8,8192]{1,0:T(8,128)(2,1)} %k_ref.1) | copy-start | bytes 393220
  69.3 26.6 %copy-start.1 = (bf16[8,8192]{1,0:T(8,128)(2,1)S(1)}, bf16[8,8192]{1,0:T(8,128)(2,1)}, u32[]{:S(2)}) copy-start(bf16[8,8192]{1,0:T(8,128)(2,1)} %v_ref.1) | copy-start | bytes 393220
  69.3 26.6 %copy-start.2 = (bf16[8,8192]{1,0:T(8,128)(2,1)S(1)}, bf16[8,8192]{1,0:T(8,128)(2,1)}, u32[]{:S(2)}) copy-start(bf16[8,8192]{1,0:T(8,128)(2,1)} %g_ref.1) | copy-start | bytes 393220

commit v5 on v4

--- a/solution.py
+++ b/solution.py
@@ -254,11 +254,11 @@
         for k in range(nblk - b):
             piece = part[:, k * 128 : k * 128 + 128]
             conv[b + k] = piece if conv[b + k] is None else conv[b + k] + piece
-    back = lax.dot_general(ahead[...], flipped[...], (((1,), (1,)), ((), ())), preferred_element_type=F32)
+    back = lax.dot_general(flipped[...], ahead[...], (((1,), (1,)), ((), ())), preferred_element_type=F32)
     for b in range(nblk):
         at = pl.ds(b * 128, 128)
         rows[0, at, :] = conv[b].T
-        rows[1, at, :] = (back[b * 128 : b * 128 + 128, :128] + back[b * 128 : b * 128 + 128, 128:]).T
+        rows[1, at, :] = back[:128, b * 128 : b * 128 + 128] + back[128:, b * 128 : b * 128 + 128]
     for q, sent in row_pieces():
         for a in range(2):
             wide[pl.ds(sent + a, NZL, stride=2), :] = rows[a, pl.ds(q, NZL, stride=NY), :]

time: 97.7 us -> 97.3 us (level)
  no operation moved by 1% of the time
where the time goes in v5:
time: 97.3 us; the launch traced here: 97 us
  blocking collectives  88.8 us (91%)
  Pallas kernels  7.45 us (8%)
    all_to_all x4, blocking collectives, exchange(): return lax.all_to_all(chunks, axes, 0, 0, tiled=True).reshape(rows.shape)  88.8 us
    pallas_call x1, Pallas kernels, group(): pl.pallas_call(group_kernel, out_shape=jax.ShapeDtypeStruct(received.shap...  3.89 us

profile of v5, /device:TPU:8, one launch (start us, length us, event | category | flops | bytes accessed | tf_op | source)
XLA Modules:
  0.0 97.0 jit_solution(7634745680686961918)
XLA Ops:
  0.6 1.9 %pack.1 = bf16[1088,128]{1,0:T(8,128)(2,1)S(1)} custom-call(bf16[8,8192]{1,0:T(8,128)(2,1)} %k_ref.1, bf16[8,8192]{1,0:T(8,128)(2,1)} %v_ref.1, bf16[8,8192]{1,0:T(8,128)(2,1)} %g_ref.1, bf16[8,8192]{1,0:T(8,128)(2,1)} %q_hbm.1, f32[16,256]{1,0:T(8,128)} %h_hbm.1), custom_call_target="tpu_custom_call" | custom-call | tf_op jit(solution)/shard_map/pack/pallas_call | solution.py:274
  2.6 33.9 %all_to_all.20 = bf16[272,4,128]{2,1,0:T(4,128)(2,1)S(1)} all-to-all(bf16[272,4,128]{2,1,0:T(4,128)(2,1)S(1)} %bitcast.15), channel_id=1, replica_groups=mesh['x'=4,'zh'=2,'core'=2,'zl'=8,'y'=4] {'zh','zl'}, dimensions={0} | all-to-all | bytes 557056 | tf_op jit(solution)/shard_map/all_to_all | solution.py:343
  36.5 0.1 inward.1
  36.6 15.0 %all_to_all.21 = bf16[320,4,128]{2,1,0:T(4,128)(2,1)S(1)} all-to-all(bf16[320,4,128]{2,1,0:T(4,128)(2,1)S(1)} %bitcast.8), channel_id=1, replica_groups=mesh['x'=4,'zh'=2,'core'=2,'zl'=8,'y'=4] {'x','core','y'}, dimensions={0} | all-to-all | bytes 655360 | tf_op jit(solution)/shard_map/all_to_all | solution.py:343
  51.6 3.9 %group.1 = bf16[1280,128]{1,0:T(8,128)(2,1)S(1)} custom-call(bf16[1280,128]{1,0:T(8,128)(2,1)S(1)} %bitcast.9), custom_call_target="tpu_custom_call" | custom-call | tf_op jit(solution)/shard_map/group/pallas_call | solution.py:324
  55.5 13.4 %all_to_all.22 = bf16[320,4,128]{2,1,0:T(4,128)(2,1)S(1)} all-to-all(bf16[320,4,128]{2,1,0:T(4,128)(2,1)S(1)} %bitcast.10), channel_id=1, replica_groups=mesh['x'=4,'zh'=2,'core'=2,'zl'=8,'y'=4] {'x','core','y'}, dimensions={0} | all-to-all | bytes 655360 | tf_op jit(solution)/shard_map/all_to_all | solution.py:343
  68.9 0.1 outward.1
  69.0 0.0 copy-start
  69.0 0.0 copy-start.1
  69.0 0.0 copy-start.2
  69.0 26.5 %all_to_all.23 = bf16[272,4,128]{2,1,0:T(4,128)(2,1)S(1)} all-to-all(bf16[272,4,128]{2,1,0:T(4,128)(2,1)S(1)} %bitcast.14), channel_id=1, replica_groups=mesh['x'=4,'zh'=2,'core'=2,'zl'=8,'y'=4] {'zh','zl'}, dimensions={0} | all-to-all | bytes 557056 | tf_op jit(solution)/shard_map/all_to_all | solution.py:343
  95.6 0.0 copy-done
  95.6 0.0 copy-done.1
  95.6 0.0 copy-done.2
  95.6 1.4 %unpack.1 = (bf16[8,8192]{1,0:T(8,128)(2,1)}, bf16[8,8192]{1,0:T(8,128)(2,1)}, bf16[8,8192]{1,0:T(8,128)(2,1)}, f32[16,256]{1,0:T(8,128)}) custom-call(bf16[1088,128]{1,0:T(8,128)(2,1)S(1)} %bitcast.12, bf16[8,8192]{1,0:T(8,128)(2,1)S(1)} %copy-done, bf16[8,8192]{1,0:T(8,128)(2,1)S(1)} %copy-done.1, bf16[8,8192]{1,0:T(8,128)(2,1)S(1)} %copy-done.2), custom_call_target="tpu_custom_call" | custom-call | tf_op jit(solution)/shard_map/unpack/pallas_call | solution.py:293
Async XLA Ops:
  69.0 26.6 %copy-start = (bf16[8,8192]{1,0:T(8,128)(2,1)S(1)}, bf16[8,8192]{1,0:T(8,128)(2,1)}, u32[]{:S(2)}) copy-start(bf16[8,8192]{1,0:T(8,128)(2,1)} %k_ref.1) | copy-start | bytes 393220
  69.0 26.6 %copy-start.1 = (bf16[8,8192]{1,0:T(8,128)(2,1)S(1)}, bf16[8,8192]{1,0:T(8,128)(2,1)}, u32[]{:S(2)}) copy-start(bf16[8,8192]{1,0:T(8,128)(2,1)} %v_ref.1) | copy-start | bytes 393220
  69.0 26.6 %copy-start.2 = (bf16[8,8192]{1,0:T(8,128)(2,1)S(1)}, bf16[8,8192]{1,0:T(8,128)(2,1)}, u32[]{:S(2)}) copy-start(bf16[8,8192]{1,0:T(8,128)(2,1)} %g_ref.1) | copy-start | bytes 393220

commit v6 on v5

--- a/solution.py
+++ b/solution.py
@@ -14,6 +14,8 @@
 NPLANE = NX * NCORE * NY
 ZROWS = 2 * NPLANE + 4
 PROWS = 2 * NZ + 8
+ZBACK = 2 * NPLANE + 2
+PBACK = 2 * NZ + 4
 Z_AXES = ("zh", "zl")
 PLANE_AXES = ("x", "core", "y")
 F32 = jnp.float32
@@ -103,12 +105,12 @@
     before[...] = r_ref[...].astype(F32)
     for j in range(NPLANE):
         for a in range(2):
-            after[pl.ds(2 * j + a, NZ, stride=ZROWS), :] = before[pl.ds(PROWS * j + a, NZ, stride=2), :]
+            after[pl.ds(2 * j + a, NZ, stride=ZBACK), :] = before[pl.ds(PBACK * j + a, NZ, stride=2), :]
     for zl in range(NZL):
-        at = pl.multiple_of((zl * NY + own) * PROWS + 2 * NZ, 8)
-        block = before[pl.ds(at, 8), :]
+        at = pl.multiple_of((zl * NY + own) * PBACK + 2 * NZ, 4)
+        block = before[pl.ds(at, 4), :]
         for zh in range(NZH):
-            after[pl.ds((zh * NZL + zl) * ZROWS + 2 * NPLANE, 4), :] = block[4 * zh : 4 * zh + 4]
+            after[pl.ds((zh * NZL + zl) * ZBACK + 2 * NPLANE, 2), :] = block[2 * zh : 2 * zh + 2]
     o_ref[...] = after[...].astype(BF16)
 
 
@@ -118,7 +120,7 @@
     for a in range(2):
         for half in range(2):
             planes = [
-                wide[pl.ds((half * TOK + i) * ZROWS + a, blocks // 2, stride=2), :] for i in range(TOK)
+                wide[pl.ds((half * TOK + i) * ZBACK + a, blocks // 2, stride=2), :] for i in range(TOK)
             ]
             for t, plane in enumerate(swap_segments(planes)):
                 tile[a, pl.ds(half * TOK + t, blocks // 2, stride=2 * TOK), :] = plane
@@ -130,25 +132,21 @@
         gk_ref[:, lanes] = (corr * v_ref[:, lanes].astype(F32)).astype(BF16)
         gv_ref[:, lanes] = (corr * k_ref[:, lanes].astype(F32)).astype(BF16)
     order = phase_order(gh_ref.shape[1], True)
-    total = None
-    for n in range(2):
-        rows = [wide[pl.ds(2 * NPLANE + 2 * n + n2, NZ, stride=ZROWS), :] for n2 in range(2)]
-        part = jnp.dot(jnp.concatenate(rows, axis=1).astype(BF16), order, preferred_element_type=F32)
-        total = part if total is None else total + part
-    gh_ref[...] = total
+    rows = [wide[pl.ds(2 * NPLANE + n, NZ, stride=ZBACK), :] for n in range(2)]
+    gh_ref[...] = jnp.dot(jnp.concatenate(rows, axis=1).astype(BF16), order, preferred_element_type=F32)
 
 
 def columns(x):
     return jnp.concatenate([x[b : b + 128].T for b in range(0, x.shape[0], 128)], axis=1)
 
 
-def row_pieces():
+def row_pieces(stride):
     for x in range(NX):
         for zh in range(NZH):
             for core in range(NCORE):
                 for y in range(NY):
                     q = (((x * NZH + zh) * NCORE + core) * NZL) * NY + y
-                    sent = ((x * NCORE + core) * NY + y) * PROWS + 2 * NZL * zh
+                    sent = ((x * NCORE + core) * NY + y) * stride + 2 * NZL * zh
                     yield q, sent
 
 
@@ -185,12 +183,10 @@
                 for d in range(4):
                     moved = pltpu.roll(column, 32 * ((d - place) % 4), 1) if place != d else column
                     spread = jnp.where((seg == d) & (row % 4 == d), moved, spread)
-                pair = [jnp.sum(spread[4 * n : 4 * n + 4], axis=0, keepdims=True) for n in range(2)]
-                high = [value.astype(BF16).astype(F32) for value in pair]
-                rows += high + [value - h for value, h in zip(pair, high)]
+                rows += [jnp.sum(spread[4 * n : 4 * n + 4], axis=0, keepdims=True) for n in range(2)]
             block = jnp.concatenate(rows, axis=0)
             for y in range(NY):
-                wide[pl.ds(((x * NCORE + core) * NY + y) * PROWS + 2 * NZ, 8), :] = block
+                wide[pl.ds(((x * NCORE + core) * NY + y) * PBACK + 2 * NZ, 4), :] = block
 
 
 def group_kernel(r_ref, o_ref, wide, rows, lhs, ahead, hi, lo, flipped):
@@ -211,7 +207,7 @@
             hi[pl.ds(p * ROWS + 8 * r, 16), :], lo[pl.ds(p * ROWS + 8 * r, 16), :] = high, low
             flipped[pl.ds(8 * r, 16), pl.ds(p * count, count)] = high
             flipped[pl.ds(ROWS + 8 * r, 16), pl.ds(p * count, count)] = low
-    for q, sent in row_pieces():
+    for q, sent in row_pieces(PROWS):
         for a in range(2):
             rows[a, pl.ds(q, NZL, stride=NY), :] = wide[pl.ds(sent + a, NZL, stride=2), :]
     sig, ups = rows[0], rows[1]
@@ -259,10 +255,10 @@
         at = pl.ds(b * 128, 128)
         rows[0, at, :] = conv[b].T
         rows[1, at, :] = back[:128, b * 128 : b * 128 + 128] + back[128:, b * 128 : b * 128 + 128]
-    for q, sent in row_pieces():
+    for q, sent in row_pieces(PBACK):
         for a in range(2):
             wide[pl.ds(sent + a, NZL, stride=2), :] = rows[a, pl.ds(q, NZL, stride=NY), :]
-    o_ref[...] = wide[...].astype(BF16)
+    o_ref[...] = wide[pl.ds(0, NPLANE * PBACK), :].astype(BF16)
 
 
 def params(mib):
@@ -293,7 +289,7 @@
     return pl.pallas_call(
         unpack_kernel,
         out_shape=(shape, shape, shape, jax.ShapeDtypeStruct(filters.shape, F32)),
-        scratch_shapes=[pltpu.VMEM((2, rows, 128), F32), pltpu.VMEM((NZ * ZROWS, 128), F32)],
+        scratch_shapes=[pltpu.VMEM((2, rows, 128), F32), pltpu.VMEM((NZ * ZBACK, 128), F32)],
         compiler_params=params(8),
         name="unpack",
     )(received, key, value, grad)
@@ -312,8 +308,8 @@
 def outward(received):
     return pl.pallas_call(
         outward_kernel,
-        out_shape=jax.ShapeDtypeStruct((NZ * ZROWS, 128), BF16),
-        scratch_shapes=[pltpu.VMEM((NPLANE * PROWS, 128), F32), pltpu.VMEM((NZ * ZROWS, 128), F32)],
+        out_shape=jax.ShapeDtypeStruct((NZ * ZBACK, 128), BF16),
+        scratch_shapes=[pltpu.VMEM((NPLANE * PBACK, 128), F32), pltpu.VMEM((NZ * ZBACK, 128), F32)],
         compiler_params=params(8),
         name="outward",
     )(received)
@@ -323,7 +319,7 @@
     count = NZ * NPLANE
     return pl.pallas_call(
         group_kernel,
-        out_shape=jax.ShapeDtypeStruct(received.shape, BF16),
+        out_shape=jax.ShapeDtypeStruct((NPLANE * PBACK, 128), BF16),
         scratch_shapes=[
             pltpu.VMEM(received.shape, F32),
             pltpu.VMEM((2, count, 128), F32),
@@ -338,8 +334,8 @@
     )(received)
 
 
-def exchange(rows, axes):
-    chunks = rows.reshape(-1, 4, 128)
+def exchange(rows, axes, unit=4):
+    chunks = rows.reshape(-1, unit, 128)
     return lax.all_to_all(chunks, axes, 0, 0, tiled=True).reshape(rows.shape)
 
 
@@ -348,7 +344,7 @@
     rows = inward(exchange(rows, Z_AXES))
     rows = group(exchange(rows, PLANE_AXES))
     rows = outward(exchange(rows, PLANE_AXES))
-    return unpack(exchange(rows, Z_AXES), key_gate, value_proj, grad_out, long_filters)
+    return unpack(exchange(rows, Z_AXES, 2), key_gate, value_proj, grad_out, long_filters)
 
 
 def solution(mesh):

time: 97.3 us -> 96.4 us (level)
  the two profiles are of different devices: /device:TPU:8 before, /device:TPU:32 now
where the time goes in v6:
time: 96.4 us; the launch traced here: 96.1 us
  blocking collectives  88 us (91%)
  Pallas kernels  7.45 us (8%)
    all_to_all x4, blocking collectives, exchange(): return lax.all_to_all(chunks, axes, 0, 0, tiled=True).reshape(rows.shape)  88 us
    pallas_call x1, Pallas kernels, group(): pl.pallas_call(group_kernel, out_shape=jax.ShapeDtypeStruct((NPLANE * PBA...  3.89 us

profile of v6, /device:TPU:32, one launch (start us, length us, event | category | flops | bytes accessed | tf_op | source)
XLA Modules:
  0.0 96.1 jit_solution(4124739779502652489)
XLA Ops:
  0.6 1.9 %pack.1 = bf16[1088,128]{1,0:T(8,128)(2,1)S(1)} custom-call(bf16[8,8192]{1,0:T(8,128)(2,1)} %k_ref.1, bf16[8,8192]{1,0:T(8,128)(2,1)} %v_ref.1, bf16[8,8192]{1,0:T(8,128)(2,1)} %g_ref.1, bf16[8,8192]{1,0:T(8,128)(2,1)} %q_hbm.1, f32[16,256]{1,0:T(8,128)} %h_hbm.1), custom_call_target="tpu_custom_call" | custom-call | tf_op jit(solution)/shard_map/pack/pallas_call | solution.py:270
  2.6 33.2 %all_to_all.20 = bf16[272,4,128]{2,1,0:T(4,128)(2,1)S(1)} all-to-all(bf16[272,4,128]{2,1,0:T(4,128)(2,1)S(1)} %bitcast.13), channel_id=1, replica_groups=mesh['x'=4,'zh'=2,'core'=2,'zl'=8,'y'=4] {'zh','zl'}, dimensions={0} | all-to-all | bytes 557056 | tf_op jit(solution)/shard_map/all_to_all | solution.py:339
  35.8 0.1 inward.1
  35.9 17.0 %all_to_all.21 = bf16[320,4,128]{2,1,0:T(4,128)(2,1)S(1)} all-to-all(bf16[320,4,128]{2,1,0:T(4,128)(2,1)S(1)} %bitcast.8), channel_id=1, replica_groups=mesh['x'=4,'zh'=2,'core'=2,'zl'=8,'y'=4] {'x','core','y'}, dimensions={0} | all-to-all | bytes 655360 | tf_op jit(solution)/shard_map/all_to_all | solution.py:339
  52.9 3.9 %group.1 = bf16[1152,128]{1,0:T(8,128)(2,1)S(1)} custom-call(bf16[1280,128]{1,0:T(8,128)(2,1)S(1)} %bitcast.9), custom_call_target="tpu_custom_call" | custom-call | tf_op jit(solution)/shard_map/group/pallas_call | solution.py:320
  56.8 13.0 %all_to_all.22 = bf16[288,4,128]{2,1,0:T(4,128)(2,1)S(1)} all-to-all(bf16[288,4,128]{2,1,0:T(4,128)(2,1)S(1)} %bitcast.10), channel_id=1, replica_groups=mesh['x'=4,'zh'=2,'core'=2,'zl'=8,'y'=4] {'x','core','y'}, dimensions={0} | all-to-all | bytes 589824 | tf_op jit(solution)/shard_map/all_to_all | solution.py:339
  69.8 0.1 outward.1
  69.9 0.0 copy-start
  69.9 0.0 copy-start.1
  69.9 0.0 copy-start.2
  69.9 24.8 %all_to_all.23 = bf16[528,2,128]{2,1,0:T(2,128)(2,1)S(1)} all-to-all(bf16[528,2,128]{2,1,0:T(2,128)(2,1)S(1)} %bitcast.14), channel_id=1, replica_groups=mesh['x'=4,'zh'=2,'core'=2,'zl'=8,'y'=4] {'zh','zl'}, dimensions={0} | all-to-all | bytes 540672 | tf_op jit(solution)/shard_map/all_to_all | solution.py:339
  94.7 0.0 copy-done
  94.7 0.0 copy-done.1
  94.7 0.0 copy-done.2
  94.7 1.4 %unpack.1 = (bf16[8,8192]{1,0:T(8,128)(2,1)}, bf16[8,8192]{1,0:T(8,128)(2,1)}, bf16[8,8192]{1,0:T(8,128)(2,1)}, f32[16,256]{1,0:T(8,128)}) custom-call(bf16[1056,128]{1,0:T(8,128)(2,1)S(1)} %bitcast.15, bf16[8,8192]{1,0:T(8,128)(2,1)S(1)} %copy-done, bf16[8,8192]{1,0:T(8,128)(2,1)S(1)} %copy-done.1, bf16[8,8192]{1,0:T(8,128)(2,1)S(1)} %copy-done.2), custom_call_target="tpu_custom_call" | custom-call | tf_op jit(solution)/shard_map/unpack/pallas_call | solution.py:289
Async XLA Ops:
  69.9 24.8 %copy-start = (bf16[8,8192]{1,0:T(8,128)(2,1)S(1)}, bf16[8,8192]{1,0:T(8,128)(2,1)}, u32[]{:S(2)}) copy-start(bf16[8,8192]{1,0:T(8,128)(2,1)} %k_ref.1) | copy-start | bytes 393220
  69.9 24.8 %copy-start.1 = (bf16[8,8192]{1,0:T(8,128)(2,1)S(1)}, bf16[8,8192]{1,0:T(8,128)(2,1)}, u32[]{:S(2)}) copy-start(bf16[8,8192]{1,0:T(8,128)(2,1)} %v_ref.1) | copy-start | bytes 393220
  69.9 24.8 %copy-start.2 = (bf16[8,8192]{1,0:T(8,128)(2,1)S(1)}, bf16[8,8192]{1,0:T(8,128)(2,1)}, u32[]{:S(2)}) copy-start(bf16[8,8192]{1,0:T(8,128)(2,1)} %g_ref.1) | copy-start | bytes 393220
